TPU v7x, 256 devices: a whole 4x4x8 slice. The times are simulated.
256 devices in a mesh: trade: 8 (over z), path: 32 (over x, y, core).
Axes of the slice: x: 4, y: 4, z: 8, core: 2. Of those that a mesh axis runs over, the one named last changes fastest.
Arguments:
- start_state: float32 [16384, 32], P('path'), may hold values from -6 to 6
- shocks: float32 [2, 16384, 32], P(None, 'path'), may hold values from -6 to 6
- loadings: float32 [32, 65536], P(None, 'trade'), may hold values from -1 to 1
- strikes: float32 [65536], P('trade'), may hold values from -0.5 to 1
- notionals: float32 [65536], P('trade'), may hold values from -1 to 1
- trade_set: int32 [65536], P('trade'), may hold values from 0 to 2047
- live_counts: int32 [8], replicated, may hold values from 1 to 8192, 49152 in all
- weights: int32 [16384], P('path'), may hold values from 1 to 16
- thresholds: int32 [2048], P('trade'), may hold values from 0 to 8
Outputs:
- exposure: float32 [2, 2048, 16384], P(None, 'trade', 'path')
- expected: float32 [2, 2048], P(None, 'trade')
Inputs may be any that keep to these rules, and one draw needn't show every extreme that they name: The live slots of group g are its first live_counts[g] slots; the counts sum to 49152 and some group is full.
All inputs are finite; a program needn't handle non-finite values.
Results may differ from a plain program's by a relative error of at most 0.0003.
Values sent between devices are 32-bit elements; how exact they have to be, the bound alone decides.
A program may use at most 128 MiB of HBM per device.

v0:
```python
import jax
import jax.numpy as jnp
from jax import lax
from jax.sharding import PartitionSpec as P

HIGHEST_PREC = lax.Precision.HIGHEST
ROOT_HALF = 0.7071067811865476


def make_basis(state):
    return jnp.concatenate([state, (state * state - 1.0) * ROOT_HALF], axis=1)


def solve_normal(gram_total, moment):
    factor = jnp.linalg.cholesky(gram_total)
    lower_solve = lax.linalg.triangular_solve(factor, moment, left_side=True, lower=True)
    return lax.linalg.triangular_solve(
        factor, lower_solve, left_side=True, lower=True, transpose_a=True
    )


def path_totals(entries):
    results = []
    for entry in entries:
        results.append(lax.psum((entry[0], entry[1]), "path"))
    return results


def body(
    start_state, shocks, loadings, strikes, notionals, trade_set, live_counts, weights, thresholds
):
    my_group = lax.axis_index("trade")
    slot_count = loadings.shape[1]
    set_count = thresholds.shape[0] * lax.axis_size("trade")
    date_count = shocks.shape[0]
    group_ids = jnp.arange(live_counts.shape[0], dtype=jnp.int32)
    filled = jnp.sum(jnp.where(group_ids == my_group, live_counts, 0))
    live = (jnp.arange(slot_count, dtype=jnp.int32) < filled).astype(jnp.float32)
    scaled = notionals * live
    weight_vals = weights.astype(jnp.float32)
    states = [start_state]
    for date_idx in range(date_count):
        states.append(0.8 * states[-1] + 0.6 * shocks[date_idx])
    bases = []
    locals_list = []
    for date_idx in range(date_count):
        basis_vals = make_basis(states[date_idx])
        weighted = basis_vals * weight_vals[:, None]
        gram_local = jnp.dot(weighted.T, basis_vals, precision=HIGHEST_PREC)
        cashflow = scaled * jnp.maximum(
            jnp.dot(states[date_idx + 1], loadings, precision=HIGHEST_PREC) - strikes, 0.0
        )
        bases.append(basis_vals)
        locals_list.append((gram_local, weighted, cashflow))
    entries = []
    for date_idx in range(date_count):
        gram_local, weighted, cashflow = locals_list[date_idx]
        entries.append((gram_local, jnp.dot(weighted.T, cashflow, precision=HIGHEST_PREC)))
    totals = path_totals(entries)
    set_coeffs = []
    for date_idx in range(date_count):
        coeffs = solve_normal(totals[date_idx][0], totals[date_idx][1])
        set_coeffs.append(jax.ops.segment_sum(coeffs.T, trade_set, num_segments=set_count))
    owned = lax.psum_scatter(jnp.stack(set_coeffs), "trade", scatter_dimension=1, tiled=True)
    netted = jnp.einsum("dnk,dpk->dnp", owned, jnp.stack(bases), precision=HIGHEST_PREC)
    limits = 0.25 * thresholds.astype(jnp.float32)
    exposure = jnp.maximum(netted - limits[None, :, None], 0.0)
    partial_sums = jnp.einsum("dnp,p->dn", exposure, weight_vals, precision=HIGHEST_PREC)
    summed, weight_total = lax.psum((partial_sums, jnp.sum(weight_vals)), "path")
    return (exposure, summed / weight_total)


def solution(mesh):
    placed = (
        P("path", None),
        P(None, "path", None),
        P(None, "trade"),
        P("trade"),
        P("trade"),
        P("trade"),
        P(),
        P("path"),
        P("trade"),
    )
    return jax.shard_map(
        body,
        mesh=mesh,
        in_specs=placed,
        out_specs=(P(None, "trade", "path"), P(None, "trade")),
        check_vma=False,
    )
```

profile of v0, /device:TPU:1, one launch (start us, length us, event | category | flops | bytes accessed | tf_op | source)
XLA Modules:
  0.0 449.4 jit_solution(11616432771246874439)
XLA Ops:
  7.2 1.0 add_multiply_fusion
  8.5 16.6 %fusion.30 = f32[512,8192]{1,0:T(8,128)} fusion(f32[32,8192]{1,0:T(8,128)S(1)} %copy-done, f32[2,512,32]{1,2,0:T(8,128)} %param.15, f32[512,32]{0,1:T(8,128)S(1)} %get-tuple-element.12), kind=kOutput, calls=%fused_computation.39 | convolution fusion | flops 1610661888 | bytes 17956864 | tf_op jit(solution)/shard_map/dot_general | solution.py:51
  25.1 15.8 %fusion.61 = f32[512,8192]{1,0:T(8,128)} fusion(f32[512,32]{0,1:T(8,128)S(1)} %get-tuple-element.12, f32[32,8192]{1,0:T(8,128)S(1)} %copy-done), kind=kOutput, calls=%fused_computation.89 | convolution fusion | flops 1610612736 | bytes 17891328 | tf_op jit(solution)/shard_map/dot_general | solution.py:51
  42.3 17.2 %fusion = f32[64,8192]{1,0:T(8,128)} fusion(f32[512,8192]{1,0:T(8,128)} %fusion.30, f32[8192]{0:T(1024)S(1)} %copy-done.4, f32[8192]{0:T(1024)S(1)} %fusion.50, f32[512,32]{0,1:T(8,128)S(1)} %get-tuple-element.11, f32[512,32]{0,1:T(8,128)S(1)} %get-tuple-element.12, f32[512]{0:T(512)S(1)} %convert_element_type.7), kind=kOutput, calls=%fused_computation.2 | convolution fusion | flops 3233873920 | bytes 19073024 | tf_op jit(solution)/shard_map/dot_general | solution.py:58
  59.5 13.0 %fusion.4 = f32[64,8192]{1,0:T(8,128)} fusion(f32[512,8192]{1,0:T(8,128)S(1)} %copy-done.1, f32[8192]{0:T(1024)S(1)} %copy-done.4, f32[8192]{0:T(1024)S(1)} %fusion.50, f32[512,32]{0,1:T(8,128)S(1)} %get-tuple-element.13, f32[512,32]{0,1:T(8,128)S(1)} %copy-done.3, f32[512]{0:T(512)S(1)} %convert_element_type.7), kind=kOutput, calls=%fused_computation.6 | convolution fusion | flops 3233873920 | bytes 19073024 | tf_op jit(solution)/shard_map/dot_general | solution.py:58
  73.1 125.0 %all-reduce.1 = (f32[64,64]{0,1:T(8,128)S(1)}, f32[64,64]{0,1:T(8,128)S(1)}) all-reduce(f32[64,64]{0,1:T(8,128)S(1)} %fusion.23, f32[64,64]{0,1:T(8,128)S(1)} %fusion.26), channel_id=1, replica_groups=mesh['trade'=8,'path'=32] {'path'}, use_global_device_ids=true, to_apply=%region_6.10 | all-reduce | flops 8192 | bytes 65536 | tf_op jit(solution)/shard_map/psum | solution.py:25
  198.3 5.8 %cholesky.55 = f32[64,64]{1,0:T(8,128)S(1)} custom-call(f32[64,64]{1,0:T(8,128)S(1)} %get-tuple-element.16), custom_call_target="Cholesky" | custom-call | tf_op jit(solution)/shard_map/jit(cholesky)/cholesky | solution.py:15
  205.5 4.9 %custom-call.13 = f32[1,64,64]{1,2,0:T(8,128)S(1)} custom-call(f32[1,64,64]{2,1,0:T(8,128)S(1)} %fusion.39), custom_call_target="InvertDiagBlocksLowerTriangular" | custom-call | tf_op jit(solution)/shard_map/triangular_solve/custom-call.2 | solution.py:17
  210.4 5.9 %cholesky.44 = f32[64,64]{1,0:T(8,128)S(1)} custom-call(f32[64,64]{1,0:T(8,128)S(1)} %get-tuple-element.17), custom_call_target="Cholesky" | custom-call | tf_op jit(solution)/shard_map/jit(cholesky)/cholesky | solution.py:15
  217.6 4.9 %custom-call.11 = f32[1,64,64]{1,2,0:T(8,128)S(1)} custom-call(f32[1,64,64]{2,1,0:T(8,128)S(1)} %fusion.38), custom_call_target="InvertDiagBlocksLowerTriangular" | custom-call | tf_op jit(solution)/shard_map/triangular_solve/custom-call.2 | solution.py:17
  222.5 3.5 fusion.40
  226.0 1.9 convolution_bitcast_fusion
  227.9 2.7 copy.16
  230.6 3.5 fusion.44
  234.1 1.9 convolution_bitcast_fusion.1
  236.1 3.0 copy.13
  239.0 44.5 %scatter_custom_fusion.1 = f32[2048,64]{1,0:T(8,128)S(1)} fusion(s32[8192]{0:T(1024)} %param.19, f32[8192,64]{1,0:T(8,128)} %copy.16, f32[]{:T(128)} %constant.49.clone.1), kind=kCustom, calls=%fused_computation.21 | custom fusion | flops 524288 | bytes 524800 | tf_op jit(solution)/shard_map/scatter-add | solution.py:63
  283.6 44.6 %scatter_custom_fusion = f32[2048,64]{1,0:T(8,128)S(1)} fusion(s32[8192]{0:T(1024)} %param.19, f32[8192,64]{1,0:T(8,128)} %copy.13, f32[]{:T(128)} %constant.49.clone.1), kind=kCustom, calls=%fused_computation.23 | custom fusion | flops 524288 | bytes 524800 | tf_op jit(solution)/shard_map/scatter-add | solution.py:63
  328.1 1.5 pad_maximum_fusion
  330.3 40.0 %reduce-scatter.2.cloned.1.call-done = f32[2,256,64]{2,1,0:T(8,128)} async-done(((f32[2,2048,64]{2,1,0:T(8,128)}), f32[2,256,64]{2,1,0:T(8,128)}) %reduce-scatter.2.cloned.1.call-update) | async-done | bytes 131088 | tf_op jit(solution)/shard_map/reduce_scatter | solution.py:64
  370.3 1.9 fusion.14
  372.3 1.0 fusion.62
  373.2 67.8 %all-reduce = (f32[2,256]{1,0:T(2,128)S(1)}, f32[]{:T(128)}) all-reduce(f32[2,256]{1,0:T(2,128)S(1)} %bitcast.59, f32[]{:T(128)} %convert_reduce_fusion), channel_id=1, replica_groups=mesh['trade'=8,'path'=32] {'path'}, use_global_device_ids=true, to_apply=%region_10.14 | all-reduce | flops 513 | bytes 4104 | tf_op jit(solution)/shard_map/psum | solution.py:69
  441.0 1.3 broadcast_divide_fusion
  (41 shorter events, 5.7 us)
Async XLA Ops:
  7.2 1.3 copy-start
  7.2 215.3 %all-reduce.5.cloned.1.call-start = ((), (), s32[]{:S(2)}) async-start(), calls=%async_computation.2 | async-start | bytes 8388608 | tf_op jit(solution)/shard_map/psum | solution.py:25
  25.1 15.9 %copy-start.6 = (s32[512]{0:T(512)S(1)}, s32[512]{0:T(512)}, u32[]{:S(2)}) copy-start(s32[512]{0:T(512)} %param.21) | copy-start | bytes 6148
  25.1 15.9 %copy-start.8 = (s32[8]{0:T(128)S(1)}, s32[8]{0:T(128)}, u32[]{:S(2)}) copy-start(s32[8]{0:T(128)} %param.20) | copy-start | bytes 100
  25.1 16.5 %copy-start.5 = (f32[8192]{0:T(1024)S(1)}, f32[8192]{0:T(1024)}, u32[]{:S(2)}) copy-start(f32[8192]{0:T(1024)} %param.18) | copy-start | bytes 98308
  25.1 17.2 %copy-start.4 = (f32[8192]{0:T(1024)S(1)}, f32[8192]{0:T(1024)}, u32[]{:S(2)}) copy-start(f32[8192]{0:T(1024)} %param.17) | copy-start | bytes 98308
  42.2 17.2 %copy-start.1 = (f32[512,8192]{1,0:T(8,128)S(1)}, f32[512,8192]{1,0:T(8,128)}, u32[]{:S(2)}) copy-start(f32[512,8192]{1,0:T(8,128)} %fusion.61) | copy-start | bytes 50331652
  42.2 17.2 %copy-start.3 = (f32[512,32]{0,1:T(8,128)S(1)}, f32[512,32]{0,1:T(8,128)}, u32[]{:S(2)}) copy-start(f32[512,32]{0,1:T(8,128)} %param.14) | copy-start | bytes 196612
  72.5 297.8 %reduce-scatter.2.cloned.1.call-start = ((), (), s32[]{:S(2)}) async-start(), calls=%async_computation.1 | async-start | bytes 2359296 | tf_op jit(solution)/shard_map/reduce_scatter | solution.py:64
  329.6 0.7 copy-start.7
  372.2 70.1 %copy-start.2 = (f32[2,256,512]{2,1,0:T(8,128)}, f32[2,256,512]{2,1,0:T(8,128)S(1)}, u32[]{:S(2)}) copy-start(f32[2,256,512]{2,1,0:T(8,128)S(1)} %fusion.14) | copy-start | bytes 3145732
Sparse Core Ops, SparseCore 0:
  72.7 125.7 all-reduce.4
  329.8 40.4 reduce-scatter.1
where the time goes:
time: 458 us; the launch traced here: 449 us
  blocking collectives  193 us (42%)
  other arithmetic  119 us (26%)
  matrix products  76.9 us (17%)
  waiting for transfers between devices  40.1 us (9%)
  between operations  14.5 us (3%)
  local copies, waits for them, and re-layouts  6.12 us (1%)
    psum x1, blocking collectives, path_totals(): results.append(lax.psum((entry[0], entry[1]), 'path'))  125 us
    scatter-add x2, other arithmetic, body(): jax.ops.segment_sum(coeffs.T, trade_set, num_segments=set_count)  89.1 us
    psum x1, blocking collectives, body(): lax.psum((partial_sums, jnp.sum(weight_vals)), 'path')  67.8 us
    reduce_scatter x1, waiting for transfers between devices, body(): lax.psum_scatter(jnp.stack(set_coeffs), 'trade', scatter_dimension=1, til...  40 us
    dot_general x2, matrix products, body(): jnp.dot(states[date_idx + 1], loadings, precision=HIGHEST_PREC) - strikes  32.4 us
    dot_general x2, matrix products, body(): jnp.dot(weighted.T, cashflow, precision=HIGHEST_PREC)  30.2 us
    another operation x6, other arithmetic, solve_normal(): factor = jnp.linalg.cholesky(gram_total)  13.1 us
    another operation x4, other arithmetic, solve_normal(): lax.linalg.triangular_solve(factor, lower_solve, left_side=True, lower=Tr...  11.1 us
  transfers between devices with their start and end apart: 2, of which 1 were waited for; matrix products, arithmetic and copies ran while one was open for 6% of the time, Pallas kernels for 0%

commit v1 on v0

v1 whole, which is shorter than its diff:
```python
import functools

import jax
import jax.numpy as jnp
from jax import lax
from jax.experimental import pallas as pl
from jax.experimental.pallas import tpu as pltpu
from jax.sharding import PartitionSpec as P

ROOT_HALF = 0.7071067811865476
F32, BF16 = jnp.float32, jnp.bfloat16
HIGHEST = lax.Precision.HIGHEST
MESH = pl.DeviceIdType.MESH
LANES = 128


def split(value):
    high = value.astype(BF16)
    return high, (value - high.astype(F32)).astype(BF16)


def dot(left, right, left_dim, right_dim, precision=None):
    return lax.dot_general(
        left, right, (((left_dim,), (right_dim,)), ((), ())), precision=precision, preferred_element_type=F32
    )


def prepare(start_ref, shocks_ref, weights_ref, state_ref, wbasis_ref, basis_ref, gram_ref):
    paths, factors = start_ref.shape
    width = 2 * factors
    dates = shocks_ref.shape[0]
    weight = weights_ref[...].astype(F32)
    state = start_ref[...].T
    wbasis_ref[...] = jnp.zeros_like(wbasis_ref)
    grams = []
    for date in range(dates):
        future = 0.8 * state + 0.6 * shocks_ref[date].T
        cols = pl.ds(date * paths, paths)
        high, low = split(future)
        state_ref[0:factors, cols] = high
        state_ref[factors : 2 * factors, cols] = high
        state_ref[2 * factors : 3 * factors, cols] = low
        row = lax.broadcasted_iota(jnp.int32, (factors, paths), 0)
        state_ref[3 * factors : 4 * factors, cols] = jnp.where(row < 3, 1.0, 0.0).astype(BF16)
        basis = jnp.concatenate([state, (state * state - 1.0) * ROOT_HALF], axis=0)
        basis_ref[date] = basis
        weighted = basis * weight
        high, low = split(weighted)
        wbasis_ref[date * width : (date + 1) * width, cols] = high
        wbasis_ref[dates * width + date * width : dates * width + (date + 1) * width, cols] = low
        grams.append(dot(weighted, basis, 1, 1, HIGHEST))
        state = future
    gram_ref[0:width, :] = jnp.concatenate(grams, axis=1)
    gram_ref[width : width + 8, :] = jnp.broadcast_to(jnp.sum(weight, axis=1, keepdims=True), (8, LANES))


def scaled_trades(loadings_ref, strikes_ref, notionals_ref, block, size):
    cols = pl.ds(pl.multiple_of(block * size, size), size)
    scale = jnp.abs(notionals_ref[:, cols])
    high, low = split(loadings_ref[:, cols] * scale)
    strike = strikes_ref[:, cols] * (-scale)
    first = strike.astype(BF16).astype(F32)
    second = (strike - first).astype(BF16).astype(F32)
    third = (strike - first) - second
    row = lax.broadcasted_iota(jnp.int32, high.shape, 0)
    parts = jnp.where(row == 0, first, jnp.where(row == 1, second, jnp.where(row == 2, third, 0.0)))
    return jnp.concatenate([high, low, high, parts.astype(BF16)], axis=0)


def moments_of(values, wbasis_ref, moment_ref, block, size):
    high, low = split(jnp.maximum(values, 0.0))
    both = dot(high, wbasis_ref[...], 1, 1)
    more = dot(low, wbasis_ref[0:LANES, :], 1, 1)
    moment = both[:, :LANES] + both[:, LANES:] + more
    high, low = split(moment)
    rows = pl.ds(pl.multiple_of(block * size, size), size)
    moment_ref[rows, 0:LANES] = high
    moment_ref[rows, LANES : 2 * LANES] = low


def local_kernel(
    size, set_size, start_ref, shocks_ref, loadings_ref, strikes_ref, notionals_ref, sets_ref, filled_ref, weights_ref,
    netted_ref, gram_ref, basis_ref, state_ref, wbasis_ref, moment_ref, values_ref, index_ref, sign_ref,
):
    slots = loadings_ref.shape[1]
    blocks = slots // size
    prepare(start_ref, shocks_ref, weights_ref, state_ref, wbasis_ref, basis_ref, gram_ref)

    def flows(block):
        return dot(scaled_trades(loadings_ref, strikes_ref, notionals_ref, block, size), state_ref[...], 0, 0)

    values_ref[0] = flows(0)

    def step(block, carry):
        values = values_ref[lax.rem(block, 2)]
        values_ref[lax.rem(block + 1, 2)] = flows(jnp.minimum(block + 1, blocks - 1))
        moments_of(values, wbasis_ref, moment_ref, block, size)
        return carry

    lax.fori_loop(0, blocks, step, 0)

    slot = lax.broadcasted_iota(jnp.int32, (1, slots), 1)
    index_ref[...] = jnp.where(slot < filled_ref[0], sets_ref[...], -1)
    notional = notionals_ref[...]
    sign_ref[...] = jnp.where(notional > 0, 1.0, jnp.where(notional < 0, -1.0, 0.0))

    def net(chunk, carry):
        row = lax.broadcasted_iota(jnp.int32, (set_size, slots), 0) + chunk * set_size
        member = jnp.where(row == index_ref[...], sign_ref[...], 0.0).astype(BF16)
        both = dot(member, moment_ref[...], 1, 0)
        rows = pl.ds(pl.multiple_of(chunk * set_size, set_size), set_size)
        netted_ref[rows, :] = both[:, :LANES] + both[:, LANES:]
        return carry

    lax.fori_loop(0, netted_ref.shape[0] // set_size, net, 0)


def local_moments(start, shocks, loadings, strikes, notionals, sets, filled, weights, set_count):
    paths, factors = start.shape
    dates = shocks.shape[0]
    slots = loadings.shape[1]
    size, set_size = min(1024, slots), min(512, set_count)
    vmem = pl.BlockSpec(memory_space=pltpu.VMEM)
    return pl.pallas_call(
        functools.partial(local_kernel, size, set_size),
        out_shape=(
            jax.ShapeDtypeStruct((set_count, LANES), F32),
            jax.ShapeDtypeStruct((2 * factors + 8, LANES), F32),
            jax.ShapeDtypeStruct((dates, 2 * factors, paths), F32),
        ),
        in_specs=[vmem] * 6 + [pl.BlockSpec(memory_space=pltpu.SMEM), vmem],
        out_specs=(vmem, vmem, vmem),
        scratch_shapes=[
            pltpu.VMEM((4 * factors, dates * paths), BF16),
            pltpu.VMEM((2 * LANES, dates * paths), BF16),
            pltpu.VMEM((slots, 2 * LANES), BF16),
            pltpu.VMEM((2, size, dates * paths), F32),
            pltpu.VMEM((1, slots), jnp.int32),
            pltpu.VMEM((1, slots), F32),
        ],
        compiler_params=pltpu.CompilerParams(vmem_limit_bytes=56 << 20),
        name="local_moments",
    )(
        start, shocks, loadings, strikes.reshape(1, -1), notionals.reshape(1, -1), sets.reshape(1, -1),
        filled.reshape(1), weights.reshape(1, -1),
    )


def invert(matrix_ref):
    size = matrix_ref.shape[0]
    lane = lax.broadcasted_iota(jnp.int32, (size, LANES), 1)
    row_id = lax.broadcasted_iota(jnp.int32, (size, LANES), 0)
    left = lane < size
    lane_row = lax.broadcasted_iota(jnp.int32, (1, LANES), 1)

    def step(j, carry):
        matrix = matrix_ref[...]
        row = matrix_ref[pl.ds(j, 1), :]

        def pick(entries, ids):
            first = jnp.sum(jnp.where(ids == j, entries, 0.0), axis=1, keepdims=True)
            second = jnp.sum(jnp.where(ids == j + size, entries, 0.0), axis=1, keepdims=True)
            return jnp.where(ids < size, first, second)

        column = pick(matrix, lane)
        inverse = 1.0 / pick(row, lane_row)
        scaled = row * inverse
        here = jnp.logical_or(lane == j, lane == j + size)
        reduced = jnp.where(here, -column * inverse, matrix - column * scaled)
        pivot_row = jnp.where(jnp.logical_or(lane_row == j, lane_row == j + size), inverse, scaled)
        matrix_ref[...] = jnp.where(row_id == j, pivot_row, reduced)
        return carry

    lax.fori_loop(0, size, step, 0)
    return left


def exchange_kernel(
    zs, xys, netted_ref, gram_ref, basis_ref, weights_ref, thresholds_ref,
    exposure_ref, expected_ref,
    gram_out, gram_in, gram_sum, gram_all, matrix_ref, core_in, plane_out, plane_in, z_out, z_in, own_ref, coeffs_ref,
    part_ref,
    gram_send, gram_recv, gall_send, gall_recv, core_send, core_recv, plane_send, plane_recv, z_send, z_recv,
    coeff_send, coeff_recv, part_send, part_recv,
):
    z = lax.axis_index("trade")
    q = lax.axis_index("path")
    xy, core = q // 2, lax.rem(q, 2)
    qs = 2 * xys
    width = basis_ref.shape[1]
    dates = basis_ref.shape[0]

    barrier = pltpu.get_barrier_semaphore()

    def greet(o, carry):
        pl.semaphore_signal(barrier, inc=1, device_id=(z, lax.rem(q + o, qs)), device_id_type=MESH)
        return carry

    lax.fori_loop(1, qs, greet, 0)

    def greet_z(o, carry):
        pl.semaphore_signal(barrier, inc=1, device_id=(lax.rem(z + o, zs), q), device_id_type=MESH)
        return carry

    lax.fori_loop(1, zs, greet_z, 0)
    pl.semaphore_wait(barrier, qs - 1 + zs - 1)

    def copy(src, dst, send, recv, device):
        return pltpu.make_async_remote_copy(
            src_ref=src, dst_ref=dst, send_sem=send, recv_sem=recv, device_id=device, device_id_type=MESH
        )

    def each(count, make, act):
        def body(o, carry):
            act(make(o))
            return carry

        lax.fori_loop(1, count, body, 0)

    other = 1 - core

    def core_copy():
        return copy(netted_ref.at[:, other], core_in, core_send, core_recv, (z, xy * 2 + other))

    core_copy().start()

    rows = width // qs

    def gram_copy(o):
        to = lax.rem(q + o, qs)
        return copy(gram_out.at[to], gram_in.at[o], gram_send.at[o], gram_recv.at[o], (z, to))

    for piece in range(qs):
        gram_out[piece, 0:rows, :] = gram_ref[piece * rows : (piece + 1) * rows, :]
        gram_out[piece, rows : rows + 1, :] = gram_ref[width : width + 1, :]
    each(qs, gram_copy, lambda c: c.start())
    gram_in[0] = gram_out[q]

    core_copy().wait()
    plane_out[...] = netted_ref[:, core] + core_in[...]

    def plane_copy(o):
        to = lax.rem(xy + o, xys)
        return copy(plane_out.at[:, to], plane_in.at[o], plane_send.at[o], plane_recv.at[o], (z, to * 2 + core))

    each(xys, plane_copy, lambda c: c.start())
    plane_in[0] = plane_out[:, xy]

    each(qs, gram_copy, lambda c: c.wait())
    gram_sum[...] = jnp.sum(gram_in[...], axis=0)

    def gall_copy(o):
        to = lax.rem(q + o, qs)
        return copy(gram_sum, gram_all.at[q], gall_send.at[o], gall_recv.at[o], (z, to))

    each(qs, gall_copy, lambda c: c.start())
    gram_all[q] = gram_sum[...]

    each(xys, plane_copy, lambda c: c.wait())
    z_out[...] = jnp.sum(plane_in[...], axis=0)

    def z_copy(o):
        to = lax.rem(z + o, zs)
        return copy(z_out.at[to], z_in.at[o], z_send.at[o], z_recv.at[o], (to, q))

    each(zs, z_copy, lambda c: c.start())
    z_in[0] = z_out[z]

    def gall_wait(o):
        return copy(gram_sum, gram_all.at[lax.rem(q + qs - o, qs)], gall_send.at[o], gall_recv.at[o], (z, q))

    each(qs, gall_copy, lambda c: c.wait_send())
    each(qs, gall_wait, lambda c: c.wait_recv())
    for piece in range(qs):
        matrix_ref[piece * rows : (piece + 1) * rows, :] = gram_all[piece, 0:rows, :]
    total = gram_all[0, rows : rows + 1, 0:1]
    left = invert(matrix_ref)
    inverse = matrix_ref[...]
    block = jnp.concatenate([jnp.where(left, inverse, 0.0), jnp.where(left, 0.0, inverse)], axis=0)

    each(zs, z_copy, lambda c: c.wait())
    moment = jnp.sum(z_in[...], axis=0)
    own_ref[...] = dot(moment, block, 1, 0, HIGHEST)

    def coeff_copy(o):
        to = lax.rem(q + o, qs)
        return copy(own_ref, coeffs_ref.at[core, xy], coeff_send.at[o], coeff_recv.at[o], (z, to))

    def coeff_wait(o):
        src = lax.rem(q + qs - o, qs)
        return copy(own_ref, coeffs_ref.at[lax.rem(src, 2), src // 2], coeff_send.at[o], coeff_recv.at[o], (z, q))

    each(qs, coeff_copy, lambda c: c.start())
    coeffs_ref[core, xy] = own_ref[...]
    weight = jnp.broadcast_to(weights_ref[...].astype(F32), (8, weights_ref.shape[1])).astype(BF16)
    sets = thresholds_ref.shape[1]
    limits = jnp.broadcast_to(0.25 * thresholds_ref[...].astype(F32), (LANES, sets)).T
    each(qs, coeff_copy, lambda c: c.wait_send())
    each(qs, coeff_wait, lambda c: c.wait_recv())

    coeffs = coeffs_ref[...].reshape(sets, LANES)
    for date in range(dates):
        netted = dot(coeffs[:, date * width : (date + 1) * width], basis_ref[date], 1, 0, HIGHEST)
        exposure = jnp.maximum(netted - limits[:, 0:1], 0.0)
        exposure_ref[date] = exposure
        high, low = split(exposure)
        part = dot(weight, high, 1, 1) + dot(weight, low, 1, 1)
        part_ref[q, date : date + 1, :] = part[0:1, :]

    def part_copy(o):
        to = lax.rem(q + o, qs)
        return copy(part_ref.at[q], part_ref.at[q], part_send.at[o], part_recv.at[o], (z, to))

    def part_wait(o):
        src = lax.rem(q + qs - o, qs)
        return copy(part_ref.at[q], part_ref.at[src], part_send.at[o], part_recv.at[o], (z, q))

    each(qs, part_copy, lambda c: c.start())
    each(qs, part_copy, lambda c: c.wait_send())
    each(qs, part_wait, lambda c: c.wait_recv())
    expected_ref[...] = jnp.sum(part_ref[...], axis=0) / total


def exchange(netted, gram, basis, weights, thresholds, zs, qs):
    xys = qs // 2
    dates, width, paths = basis.shape
    sets = thresholds.shape[0]
    per = sets // qs
    tall = (width // qs + 8) // 8 * 8
    vmem = pl.BlockSpec(memory_space=pltpu.VMEM)
    dma = pltpu.SemaphoreType.DMA
    return pl.pallas_call(
        functools.partial(exchange_kernel, zs, xys),
        out_shape=(
            jax.ShapeDtypeStruct((dates, sets, paths), F32),
            jax.ShapeDtypeStruct((dates, sets), F32),
        ),
        in_specs=[vmem] * 5,
        out_specs=(vmem, vmem),
        scratch_shapes=[
            pltpu.VMEM((qs, tall, LANES), F32),
            pltpu.VMEM((qs, tall, LANES), F32),
            pltpu.VMEM((tall, LANES), F32),
            pltpu.VMEM((qs, tall, LANES), F32),
            pltpu.VMEM((width, LANES), F32),
            pltpu.VMEM((zs, xys, per, LANES), F32),
            pltpu.VMEM((zs, xys, per, LANES), F32),
            pltpu.VMEM((xys, zs, per, LANES), F32),
            pltpu.VMEM((zs, per, LANES), F32),
            pltpu.VMEM((zs, per, LANES), F32),
            pltpu.VMEM((per, LANES), F32),
            pltpu.VMEM((2, xys, per, LANES), F32),
            pltpu.VMEM((qs, dates, sets), F32),
            dma((qs,)), dma((qs,)), dma((qs,)), dma((qs,)), dma, dma, dma((xys,)), dma((xys,)), dma((zs,)), dma((zs,)),
            dma((qs,)), dma((qs,)), dma((qs,)), dma((qs,)),
        ],
        compiler_params=pltpu.CompilerParams(
            collective_id=0, has_side_effects=True, vmem_limit_bytes=48 << 20
        ),
        name="exchange",
    )(netted.reshape(zs, 2, xys, per, LANES), gram, basis, weights.reshape(1, -1), thresholds.reshape(1, -1))


def body(
    start_state, shocks, loadings, strikes, notionals, trade_set, live_counts, weights, thresholds
):
    zs, qs = lax.axis_size("trade"), lax.axis_size("path")
    filled = live_counts[lax.axis_index("trade")]
    netted, gram, basis = local_moments(
        start_state, shocks, loadings, strikes, notionals, trade_set, filled, weights, thresholds.shape[0] * zs
    )
    return exchange(netted, gram, basis, weights, thresholds, zs, qs)


def solution(mesh):
    placed = (
        P("path", None),
        P(None, "path", None),
        P(None, "trade"),
        P("trade"),
        P("trade"),
        P("trade"),
        P(),
        P("path"),
        P("trade"),
    )
    return jax.shard_map(
        body,
        mesh=mesh,
        in_specs=placed,
        out_specs=(P(None, "trade", "path"), P(None, "trade")),
        check_vma=False,
    )
```

time: 458 us -> 87.4 us (0.19); the launches traced: 449 us -> 87.1 us
  blocking collectives: 193 us -> 0 us
  other arithmetic: 119 us -> 0 us
  Pallas kernels: 0 us -> 77.3 us
  matrix products: 76.9 us -> 0 us
  waiting for transfers between devices: 40.1 us -> 0 us
  between operations: 14.5 us -> 0.66 us
    psum x2 -> x0, blocking collectives: 193 us -> none  [the longest x1 125 us: path_totals(): results.append(lax.psum((entry[0], entry[1]), 'path'))]
    scatter-add x2 -> x0, other arithmetic: 89.1 us -> none  [body(): jax.ops.segment_sum(coeffs.T, trade_set, num_segments=set_count)]
    pallas_call x0 -> x2, Pallas kernels: none -> 77.3 us  [the longest x1 45.1 us: exchange(): pl.pallas_call(functools.partial(exchange_kernel, zs, xys), out_shape=(ja...]
    dot_general x8 -> x0, matrix products: 66.1 us -> none  [the longest x2 32.4 us: body(): jnp.dot(states[date_idx + 1], loadings, precision=HIGHEST_PREC) - strikes]
    reduce_scatter x1 -> x0, waiting for transfers between devices: 40 us -> none  [body(): lax.psum_scatter(jnp.stack(set_coeffs), 'trade', scatter_dimension=1, til...]
    another operation x12 -> x0, other arithmetic: 25.7 us -> none  [the longest x6 13.1 us: solve_normal(): factor = jnp.linalg.cholesky(gram_total)]
    another operation x4 -> x0, matrix products: 10.8 us -> none  [the longest x2 6.97 us: solve_normal(): lax.linalg.triangular_solve(factor, moment, left_side=True, lower=True)]
    unnamed x18, local copies, waits for them, and re-layouts: 0.32 us -> 8.56 us
  transfers between devices with their start and end apart: 2 -> 0, of which waited for: 1 -> 0; matrix products, arithmetic and copies ran while one was open for 6% -> 0% of each run, Pallas kernels for 0% -> 0%
where the time goes in v1:
time: 87.4 us; the launch traced here: 87.1 us
  Pallas kernels  77.3 us (88%)
  local copies, waits for them, and re-layouts  9.14 us (10%)
    pallas_call x1, Pallas kernels, exchange(): pl.pallas_call(functools.partial(exchange_kernel, zs, xys), out_shape=(ja...  45.1 us
    pallas_call x1, Pallas kernels, local_moments(): pl.pallas_call(functools.partial(local_kernel, size, set_size), out_shape...  32.1 us
    unnamed x18, local copies, waits for them, and re-layouts  8.56 us

profile of v1, /device:TPU:1, one launch (start us, length us, event | category | flops | bytes accessed | tf_op | source)
XLA Modules:
  0.0 87.1 jit_solution(15043049366165518789)
XLA Ops:
  0.6 0.0 copy-start.6
  0.6 0.6 copy-done.6
  1.3 0.6 dynamic_slice.3.filled_ref
  1.9 0.0 copy-start.5
  1.9 1.7 %copy.11.start_ref = f32[512,32]{1,0:T(8,128)} copy(f32[512,32]{0,1:T(8,128)} %param.9) | data formatting | bytes 131072 | tf_op args[0]
  3.6 0.0 copy-done.5
  3.6 1.0 %copy.12.shocks_ref = f32[2,512,32]{2,1,0:T(8,128)} copy(f32[2,512,32]{1,2,0:T(8,128)S(1)} %copy-done.5) | data formatting | bytes 262144 | tf_op args[1]
  4.6 32.1 %local_moments.1 = (f32[2048,128]{1,0:T(8,128)}, f32[72,128]{1,0:T(8,128)}, f32[2,64,512]{2,1,0:T(8,128)}) custom-call(f32[512,32]{1,0:T(8,128)} %copy.11.start_ref, f32[2,512,32]{2,1,0:T(8,128)} %copy.12.shocks_ref, f32[32,8192]{1,0:T(8,128)} %loadings_ref.1, f32[1,8192]{1,0:T(1,128)} %bitcast.10, f32[1,8192]{1,0:T(1,128)} %bitcast.11, s32[1,8192]{1,0:T(1,128)} %bitcast.12, ...), custom_call_target="tpu_custom_call" | custom-call | tf_op jit(solution)/shard_map/local_moments/pallas_call | solution.py:124
  36.7 0.0 copy-start.3
  36.7 0.0 copy-start.4
  36.7 0.7 copy-done.3
  37.4 0.0 copy-done.4
  37.4 0.0 copy-start
  37.4 1.2 %copy-done = f32[2048,128]{1,0:T(8,128)S(1)} copy-done((f32[2048,128]{1,0:T(8,128)S(1)}, f32[2048,128]{1,0:T(8,128)}, u32[]{:S(2)}) %copy-start) | copy-done | bytes 1048600
  38.7 0.0 copy-start.1
  38.7 0.9 %copy-done.1 = f32[2,64,512]{2,1,0:T(8,128)S(1)} copy-done((f32[2,64,512]{2,1,0:T(8,128)S(1)}, f32[2,64,512]{2,1,0:T(8,128)}, u32[]{:S(2)}) %copy-start.1) | copy-done | bytes 262168
  39.6 0.0 copy-start.2
  39.6 0.8 copy-done.2
  40.4 45.1 %exchange.1 = (f32[2,256,512]{2,1,0:T(8,128)S(1)}, f32[2,256]{1,0:T(2,128)S(1)}) custom-call(f32[8,2,16,8,128]{4,3,2,1,0:T(8,128)S(1)} %bitcast.6, f32[72,128]{1,0:T(8,128)S(1)} %copy-done.2, f32[2,64,512]{2,1,0:T(8,128)S(1)} %copy-done.1, s32[1,512]{1,0:T(1,128)S(1)} %bitcast.8, s32[1,256]{1,0:T(1,128)S(1)} %bitcast.9), custom_call_target="tpu_custom_call" | custom-call | tf_op jit(solution)/shard_map/exchange/pallas_call | solution.py:332
  85.5 1.0 %copy.15 = f32[2,256,512]{2,1,0:T(8,128)} copy(f32[2,256,512]{2,1,0:T(8,128)S(1)} %get-tuple-element.10) | data formatting | bytes 2097152
  86.5 0.6 copy.16
Async XLA Ops:
  0.6 0.7 copy-start.6
  1.9 1.7 %copy-start.5 = (f32[2,512,32]{1,2,0:T(8,128)S(1)}, f32[2,512,32]{1,2,0:T(8,128)}, u32[]{:S(2)}) copy-start(f32[2,512,32]{1,2,0:T(8,128)} %param.10) | copy-start | bytes 393220
  36.7 0.7 copy-start.3
  36.7 0.7 copy-start.4
  37.4 1.2 %copy-start = (f32[2048,128]{1,0:T(8,128)S(1)}, f32[2048,128]{1,0:T(8,128)}, u32[]{:S(2)}) copy-start(f32[2048,128]{1,0:T(8,128)} %get-tuple-element.5) | copy-start | bytes 3145732
  38.7 0.9 %copy-start.1 = (f32[2,64,512]{2,1,0:T(8,128)S(1)}, f32[2,64,512]{2,1,0:T(8,128)}, u32[]{:S(2)}) copy-start(f32[2,64,512]{2,1,0:T(8,128)} %get-tuple-element.7.basis_ref) | copy-start | bytes 786436
  39.6 0.8 copy-start.2

commit v2 on v0

v2 whole, which is shorter than its diff:
```python
import functools

import jax
import jax.numpy as jnp
from jax import lax
from jax.experimental import pallas as pl
from jax.experimental.pallas import tpu as pltpu
from jax.sharding import PartitionSpec as P

ROOT_HALF = 0.7071067811865476
F32, BF16 = jnp.float32, jnp.bfloat16
HIGHEST = lax.Precision.HIGHEST
MESH = pl.DeviceIdType.MESH
LANES = 128


def split(value):
    high = value.astype(BF16)
    return high, (value - high.astype(F32)).astype(BF16)


def dot(left, right, left_dim, right_dim, precision=None):
    return lax.dot_general(
        left, right, (((left_dim,), (right_dim,)), ((), ())), precision=precision, preferred_element_type=F32
    )


def make_basis(state):
    return jnp.concatenate([state, (state * state - 1.0) * ROOT_HALF], axis=0)


def scaled_trades(loadings_ref, strikes_ref, notionals_ref, block, size):
    cols = pl.ds(pl.multiple_of(block * size, size), size)
    scale = jnp.abs(notionals_ref[:, cols])
    high, low = split(loadings_ref[:, cols] * scale)
    strike = strikes_ref[:, cols] * (-scale)
    first = strike.astype(BF16).astype(F32)
    second = (strike - first).astype(BF16).astype(F32)
    third = (strike - first) - second
    row = lax.broadcasted_iota(jnp.int32, high.shape, 0)
    parts = jnp.where(row == 0, first, jnp.where(row == 1, second, jnp.where(row == 2, third, 0.0)))
    return jnp.concatenate([high, low, high, parts.astype(BF16)], axis=0)


def invert_steps(matrix_ref, begin, end):
    size = matrix_ref.shape[0]
    lane = lax.broadcasted_iota(jnp.int32, (size, LANES), 1)
    row_id = lax.broadcasted_iota(jnp.int32, (size, LANES), 0)
    lane_row = lax.broadcasted_iota(jnp.int32, (1, LANES), 1)

    def step(j, carry):
        matrix = matrix_ref[...]
        row = matrix_ref[pl.ds(j, 1), :]

        def pick(entries, ids):
            first = jnp.sum(jnp.where(ids == j, entries, 0.0), axis=1, keepdims=True)
            second = jnp.sum(jnp.where(ids == j + size, entries, 0.0), axis=1, keepdims=True)
            return jnp.where(ids < size, first, second)

        column = pick(matrix, lane)
        inverse = 1.0 / pick(row, lane_row)
        scaled = row * inverse
        here = jnp.logical_or(lane == j, lane == j + size)
        reduced = jnp.where(here, -column * inverse, matrix - column * scaled)
        pivot_row = jnp.where(jnp.logical_or(lane_row == j, lane_row == j + size), inverse, scaled)
        matrix_ref[...] = jnp.where(row_id == j, pivot_row, reduced)
        return carry

    lax.fori_loop(begin, end, step, 0)


def loop(begin, end, act):
    def step(i, carry):
        act(i)
        return carry

    lax.fori_loop(begin, end, step, 0)


def kernel(
    zs, xys, size,
    start_ref, shocks_ref, weights_ref, thresholds_ref, counts_ref, loadings_hbm, strikes_hbm, notionals_hbm, sets_hbm,
    exposure_ref, expected_ref,
    loadings_ref, strikes_ref, notionals_ref, sets_ref, local_sem,
    own_states, other_states, state_ref, wbasis_ref, basis_ref, moment_ref,
    gram_out, gram_in, gram_sum, gram_all, matrix_ref,
    net_ref, core_in, plane_out, plane_in, z_out, z_in, own_ref, coeffs_ref, part_ref,
    state_send, state_recv, gram_send, gram_recv, gall_send, gall_recv, core_send, core_recv, plane_send, plane_recv,
    z_send, z_recv, coeff_send, coeff_recv, part_send, part_recv,
):
    z = lax.axis_index("trade")
    q = lax.axis_index("path")
    xy, core = q // 2, lax.rem(q, 2)
    other = 1 - core
    qs = 2 * xys
    factors, paths = start_ref.shape
    dates = shocks_ref.shape[0]
    width = 2 * factors
    slots = loadings_ref.shape[1]
    chunks = core_send.shape[0]
    per_chunk = zs // chunks
    set_count = per_chunk * thresholds_ref.shape[1]

    def copy(src, dst, send, recv, device):
        return pltpu.make_async_remote_copy(
            src_ref=src, dst_ref=dst, send_sem=send, recv_sem=recv, device_id=device, device_id_type=MESH
        )

    half = pl.ds(pl.multiple_of(core * slots, slots), slots)
    fetches = [
        pltpu.make_async_copy(hbm.at[:, half], ref, local_sem.at[i])
        for i, (hbm, ref) in enumerate(
            [
                (loadings_hbm, loadings_ref),
                (strikes_hbm, strikes_ref),
                (notionals_hbm, notionals_ref),
                (sets_hbm, sets_ref),
            ]
        )
    ]
    for fetch in fetches:
        fetch.start()

    barrier = pltpu.get_barrier_semaphore()

    def greet(device):
        pl.semaphore_signal(barrier, inc=1, device_id=device, device_id_type=MESH)

    loop(1, qs, lambda o: greet((z, lax.rem(q + o, qs))))
    loop(1, zs, lambda o: greet((lax.rem(z + o, zs), q)))

    weight = jnp.broadcast_to(weights_ref[...].astype(F32), (8, paths))
    state = start_ref[...]
    own_states[0:factors, :] = state
    for date in range(dates):
        state = 0.8 * state + 0.6 * shocks_ref[date]
        own_states[(date + 1) * factors : (date + 2) * factors, :] = state
    bottom = (dates + 1) * factors
    own_states[bottom : bottom + 8, :] = weight

    pl.semaphore_wait(barrier, qs - 1 + zs - 1)
    states_copy = copy(own_states, other_states, state_send, state_recv, (z, xy * 2 + other))
    states_copy.start()

    def prepare(states, place):
        cols = pl.ds(place * paths, paths)
        scale = states[bottom : bottom + 1, :]
        grams = []
        for date in range(dates):
            basis = make_basis(states[date * factors : (date + 1) * factors, :])
            weighted = basis * scale
            high, low = split(weighted)
            wbasis_ref[date, 0:width, cols] = high
            wbasis_ref[date, width : 2 * width, cols] = low
            grams.append(dot(weighted, basis, 1, 1, HIGHEST))
            future = states[(date + 1) * factors : (date + 2) * factors, :]
            high = future.astype(BF16).astype(F32)
            ones = jnp.where(lax.broadcasted_iota(jnp.int32, future.shape, 0) < 3, 1.0, 0.0)
            rows = jnp.concatenate([high, high, future - high, ones], axis=0)
            state_ref[date, cols, :] = rows.T.astype(BF16)
            if place == 0:
                high, low = split(basis)
                zero = jnp.zeros_like(high)
                for part, entries in enumerate((high, high, low)):
                    for k in range(dates):
                        at = part * dates * width + k * width
                        basis_ref[date, at : at + width, :] = entries if k == date else zero
        return jnp.concatenate(grams, axis=1), jnp.sum(scale, axis=1, keepdims=True)

    gram, total = prepare(own_states, 0)
    states_copy.wait_recv()
    more, more_total = prepare(other_states, 1)
    gram = gram + more
    total = total + more_total

    rows = width // xys
    for piece in range(xys):
        gram_out[piece, 0:rows, :] = gram[piece * rows : (piece + 1) * rows, :]
        gram_out[piece, rows : rows + 1, :] = jnp.broadcast_to(total, (1, LANES))

    def plane_device(o):
        return (z, lax.rem(xy + o, xys) * 2 + core)

    def gram_copy(o):
        return copy(gram_out.at[lax.rem(xy + o, xys)], gram_in.at[o], gram_send.at[o], gram_recv.at[o], plane_device(o))

    loop(1, xys, lambda o: gram_copy(o).start())
    gram_in[0] = gram_out[xy]

    for fetch in fetches:
        fetch.wait()

    def moments(block):
        trades = scaled_trades(loadings_ref, strikes_ref, notionals_ref, block, size)
        cols = pl.ds(pl.multiple_of(block * size, size), size)
        for date in range(dates):
            flows = jnp.maximum(dot(state_ref[date], trades, 1, 0), 0.0)
            high, low = split(flows)
            both = dot(wbasis_ref[date], high, 1, 0)
            least = dot(wbasis_ref[date, 0:width, :], low, 1, 0)
            high, low = split(both[0:width] + both[width:] + least)
            moment_ref[date * width : (date + 1) * width, cols] = high
            moment_ref[LANES + date * width : LANES + (date + 1) * width, cols] = low

    loop(0, slots // size, moments)

    loop(1, xys, lambda o: gram_copy(o).wait_recv())
    gram_sum[...] = jnp.sum(gram_in[...], axis=0)

    def gall_copy(o):
        return copy(gram_sum, gram_all.at[xy], gall_send.at[o], gall_recv.at[o], plane_device(o))

    def gall_wait(o):
        return copy(gram_sum, gram_all.at[lax.rem(xy + xys - o, xys)], gall_send.at[o], gall_recv.at[o], plane_device(o))

    loop(1, xys, lambda o: gall_copy(o).start())
    gram_all[xy] = gram_sum[...]

    slot = core * slots + lax.broadcasted_iota(jnp.int32, (1, slots), 1)
    sets_ref[...] = jnp.where(slot < counts_ref[z], sets_ref[...], -1)
    notional = notionals_ref[...]
    notionals_ref[...] = jnp.where(notional > 0, 1.0, jnp.where(notional < 0, -1.0, 0.0))

    def owners(chunk):
        return pl.ds(chunk * per_chunk, per_chunk)

    def core_copy(chunk):
        return copy(
            net_ref.at[owners(chunk), other],
            core_in.at[owners(chunk)],
            core_send.at[chunk],
            core_recv.at[chunk],
            (z, xy * 2 + other),
        )

    def plane_copy(chunk, o):
        return copy(
            plane_out.at[owners(chunk), lax.rem(xy + o, xys)],
            plane_in.at[o, owners(chunk)],
            plane_send.at[chunk, o],
            plane_recv.at[chunk, o],
            plane_device(o),
        )

    def to_plane(chunk):
        core_copy(chunk).wait_recv()
        plane_out[owners(chunk)] = net_ref[owners(chunk), core] + core_in[owners(chunk)]
        loop(1, xys, lambda o: plane_copy(chunk, o).start())
        plane_in[0, owners(chunk)] = plane_out[owners(chunk), xy]

    def net(chunk):
        row = lax.broadcasted_iota(jnp.int32, (set_count, slots), 0) + chunk * set_count
        member = jnp.where(row == sets_ref[...], notionals_ref[...], 0.0).astype(BF16)
        both = dot(member, moment_ref[...], 1, 1)
        net_ref[owners(chunk)] = (both[:, :LANES] + both[:, LANES:]).reshape(per_chunk, *net_ref.shape[1:])
        core_copy(chunk).start()

        @pl.when(chunk > 0)
        def _():
            to_plane(chunk - 1)

    loop(0, chunks, net)
    to_plane(chunks - 1)

    def z_copy(to):
        return copy(z_out.at[to], z_in.at[z], z_send.at[to], z_recv.at[z], (to, q))

    def z_wait(src):
        return copy(z_out.at[src], z_in.at[src], z_send.at[src], z_recv.at[src], (src, q))

    def others(act):
        def one(to):
            @pl.when(to != z)
            def _():
                act(to)

        return one

    def to_z(chunk):
        loop(1, xys, lambda o: plane_copy(chunk, o).wait_recv())
        z_out[owners(chunk)] = jnp.sum(plane_in[:, owners(chunk)], axis=0)
        loop(chunk * per_chunk, (chunk + 1) * per_chunk, others(lambda to: z_copy(to).start()))

    loop(0, chunks - 1, to_z)
    loop(1, xys, lambda o: gall_wait(o).wait_recv())
    for piece in range(xys):
        matrix_ref[piece * rows : (piece + 1) * rows, :] = gram_all[piece, 0:rows, :]
    invert_steps(matrix_ref, 0, width // 2)
    to_z(chunks - 1)
    z_in[z] = z_out[z]
    invert_steps(matrix_ref, width // 2, width)
    inverse = matrix_ref[...]
    left = lax.broadcasted_iota(jnp.int32, inverse.shape, 1) < width
    block = jnp.concatenate([jnp.where(left, inverse, 0.0), jnp.where(left, 0.0, inverse)], axis=0)
    loop(0, zs, others(lambda src: z_wait(src).wait_recv()))
    own_ref[...] = dot(jnp.sum(z_in[...], axis=0), block, 1, 0, HIGHEST)

    def any_device(o):
        return (z, lax.rem(q + o, qs))

    def coeff_copy(o):
        return copy(own_ref, coeffs_ref.at[core, xy], coeff_send.at[o], coeff_recv.at[o], any_device(o))

    def coeff_wait(o):
        src = lax.rem(q + qs - o, qs)
        return copy(
            own_ref, coeffs_ref.at[lax.rem(src, 2), src // 2], coeff_send.at[o], coeff_recv.at[o], any_device(o)
        )

    loop(1, qs, lambda o: coeff_copy(o).start())
    coeffs_ref[core, xy] = own_ref[...]
    sets = thresholds_ref.shape[1]
    limits = jnp.broadcast_to(0.25 * thresholds_ref[...].astype(F32), (LANES, sets)).T
    loop(1, qs, lambda o: coeff_wait(o).wait_recv())

    high, low = split(coeffs_ref[...].reshape(sets, LANES))
    coeffs = jnp.concatenate([high, low, high], axis=1)
    weight = weight.astype(BF16)
    for date in range(dates):
        exposure = jnp.maximum(dot(coeffs, basis_ref[date], 1, 0) - limits[:, 0:1], 0.0)
        exposure_ref[date] = exposure
        high, low = split(exposure)
        part = dot(weight, high, 1, 1) + dot(weight, low, 1, 1)
        part_ref[q, date : date + 1, :] = part[0:1, :]

    def part_copy(o):
        return copy(part_ref.at[q], part_ref.at[q], part_send.at[o], part_recv.at[o], any_device(o))

    def part_wait(o):
        src = lax.rem(q + qs - o, qs)
        return copy(part_ref.at[q], part_ref.at[src], part_send.at[o], part_recv.at[o], any_device(o))

    loop(1, qs, lambda o: part_copy(o).start())
    states_copy.wait_send()
    loop(1, xys, lambda o: gram_copy(o).wait_send())
    loop(1, xys, lambda o: gall_copy(o).wait_send())
    loop(0, chunks, lambda chunk: core_copy(chunk).wait_send())
    loop(0, chunks, lambda chunk: loop(1, xys, lambda o: plane_copy(chunk, o).wait_send()))
    loop(0, zs, others(lambda to: z_copy(to).wait_send()))
    loop(1, qs, lambda o: coeff_copy(o).wait_send())
    loop(1, qs, lambda o: part_wait(o).wait_recv())
    expected_ref[...] = jnp.sum(part_ref[...], axis=0) / gram_all[0, rows : rows + 1, 0:1]
    loop(1, qs, lambda o: part_copy(o).wait_send())


def body(
    start_state, shocks, loadings, strikes, notionals, trade_set, live_counts, weights, thresholds
):
    zs, qs = lax.axis_size("trade"), lax.axis_size("path")
    xys = qs // 2
    paths, factors = start_state.shape
    dates = shocks.shape[0]
    width = 2 * factors
    slots = loadings.shape[1] // 2
    size = min(1024, slots)
    sets = thresholds.shape[0]
    per = sets // qs
    chunks = 4 if zs % 4 == 0 else zs
    tall = (width // xys + 8) // 8 * 8
    vmem = pl.BlockSpec(memory_space=pltpu.VMEM)
    hbm = pl.BlockSpec(memory_space=pl.ANY)
    dma = pltpu.SemaphoreType.DMA
    return pl.pallas_call(
        functools.partial(kernel, zs, xys, size),
        out_shape=(
            jax.ShapeDtypeStruct((dates, sets, paths), F32),
            jax.ShapeDtypeStruct((dates, sets), F32),
        ),
        in_specs=[vmem] * 4 + [pl.BlockSpec(memory_space=pltpu.SMEM)] + [hbm] * 4,
        out_specs=(vmem, vmem),
        scratch_shapes=[
            pltpu.VMEM((factors, slots), F32),
            pltpu.VMEM((1, slots), F32),
            pltpu.VMEM((1, slots), F32),
            pltpu.VMEM((1, slots), jnp.int32),
            dma((4,)),
            pltpu.VMEM(((dates + 1) * factors + 8, paths), F32),
            pltpu.VMEM(((dates + 1) * factors + 8, paths), F32),
            pltpu.VMEM((dates, 2 * paths, 4 * factors), BF16),
            pltpu.VMEM((dates, 2 * width, 2 * paths), BF16),
            pltpu.VMEM((dates, 3 * dates * width, paths), BF16),
            pltpu.VMEM((2 * LANES, slots), BF16),
            pltpu.VMEM((xys, tall, LANES), F32),
            pltpu.VMEM((xys, tall, LANES), F32),
            pltpu.VMEM((tall, LANES), F32),
            pltpu.VMEM((xys, tall, LANES), F32),
            pltpu.VMEM((width, LANES), F32),
            pltpu.VMEM((zs, 2, xys, per, LANES), F32),
            pltpu.VMEM((zs, xys, per, LANES), F32),
            pltpu.VMEM((zs, xys, per, LANES), F32),
            pltpu.VMEM((xys, zs, per, LANES), F32),
            pltpu.VMEM((zs, per, LANES), F32),
            pltpu.VMEM((zs, per, LANES), F32),
            pltpu.VMEM((per, LANES), F32),
            pltpu.VMEM((2, xys, per, LANES), F32),
            pltpu.VMEM((qs, dates, sets), F32),
            dma, dma, dma((xys,)), dma((xys,)), dma((xys,)), dma((xys,)), dma((chunks,)), dma((chunks,)),
            dma((chunks, xys)), dma((chunks, xys)), dma((zs,)), dma((zs,)), dma((qs,)), dma((qs,)), dma((qs,)), dma((qs,)),
        ],
        compiler_params=pltpu.CompilerParams(
            collective_id=0, has_side_effects=True, vmem_limit_bytes=56 << 20
        ),
        name="exposures",
    )(
        start_state.T, shocks.transpose(0, 2, 1), weights.reshape(1, -1), thresholds.reshape(1, -1), live_counts,
        loadings, strikes.reshape(1, -1), notionals.reshape(1, -1), trade_set.reshape(1, -1),
    )


def solution(mesh):
    placed = (
        P("path", None),
        P(None, "path", None),
        P(None, "trade"),
        P("trade"),
        P("trade"),
        P("trade"),
        P(),
        P("path"),
        P("trade"),
    )
    return jax.shard_map(
        body,
        mesh=mesh,
        in_specs=placed,
        out_specs=(P(None, "trade", "path"), P(None, "trade")),
        check_vma=False,
    )
```

time: 458 us -> 62.1 us (0.14); the launches traced: 449 us -> 62 us
  blocking collectives: 193 us -> 0 us
  other arithmetic: 119 us -> 0 us
  matrix products: 76.9 us -> 0 us
  Pallas kernels: 0 us -> 58.5 us
  waiting for transfers between devices: 40.1 us -> 0 us
  between operations: 14.5 us -> 0.65 us
    psum x2 -> x0, blocking collectives: 193 us -> none  [the longest x1 125 us: path_totals(): results.append(lax.psum((entry[0], entry[1]), 'path'))]
    scatter-add x2 -> x0, other arithmetic: 89.1 us -> none  [body(): jax.ops.segment_sum(coeffs.T, trade_set, num_segments=set_count)]
    dot_general x8 -> x0, matrix products: 66.1 us -> none  [the longest x2 32.4 us: body(): jnp.dot(states[date_idx + 1], loadings, precision=HIGHEST_PREC) - strikes]
    pallas_call x0 -> x1, Pallas kernels: none -> 58.5 us  [body(): pl.pallas_call(functools.partial(kernel, zs, xys, size), out_shape=(jax.S...]
    reduce_scatter x1 -> x0, waiting for transfers between devices: 40 us -> none  [body(): lax.psum_scatter(jnp.stack(set_coeffs), 'trade', scatter_dimension=1, til...]
    another operation x12 -> x0, other arithmetic: 25.7 us -> none  [the longest x6 13.1 us: solve_normal(): factor = jnp.linalg.cholesky(gram_total)]
    another operation x4 -> x0, matrix products: 10.8 us -> none  [the longest x2 6.97 us: solve_normal(): lax.linalg.triangular_solve(factor, moment, left_side=True, lower=True)]
    transpose x2 -> x0, local copies, waits for them, and re-layouts: 5.65 us -> none  [body(): set_coeffs.append(jax.ops.segment_sum(coeffs.T, trade_set, num_segments=s...]
  transfers between devices with their start and end apart: 2 -> 0, of which waited for: 1 -> 0; matrix products, arithmetic and copies ran while one was open for 6% -> 0% of each run, Pallas kernels for 0% -> 0%
where the time goes in v2:
time: 62.1 us; the launch traced here: 62 us
  Pallas kernels  58.5 us (94%)
  local copies, waits for them, and re-layouts  2.85 us (5%)
  between operations  0.65 us (1%)
    pallas_call x1, Pallas kernels, body(): pl.pallas_call(functools.partial(kernel, zs, xys, size), out_shape=(jax.S...  58.5 us
    unnamed x4, local copies, waits for them, and re-layouts  2.85 us

profile of v2, /device:TPU:1, one launch (start us, length us, event | category | flops | bytes accessed | tf_op | source)
XLA Modules:
  0.0 62.0 jit_solution(10064901234135363272)
XLA Ops:
  0.6 58.5 %exposures.1 = (f32[2,256,512]{2,1,0:T(8,128)}, f32[2,256]{1,0:T(2,128)}) custom-call(f32[32,512]{1,0:T(8,128)} %bitcast.8, f32[2,32,512]{2,1,0:T(8,128)} %bitcast.7, s32[1,512]{1,0:T(1,128)} %bitcast.12, s32[1,256]{1,0:T(1,128)} %bitcast.13, s32[8]{0:T(128)} %counts_ref.1, f32[32,8192]{1,0:T(8,128)} %loadings_hbm.1, f32[1,8192]{1,0:T(1,128)} %bitcast.9, ...), custom_call_target="tpu_custom_call" | custom-call | tf_op jit(solution)/shard_map/exposures/pallas_call | solution.py:363
  59.1 0.0 copy-start
  59.2 2.3 %copy.13 = f32[2,256,512]{2,1,0:T(8,128)} copy(f32[2,256,512]{2,1,0:T(8,128)} %get-tuple-element.4) | data formatting | bytes 2097152
  61.4 0.0 copy-done
  61.4 0.6 copy.14
Async XLA Ops:
  59.1 2.3 %copy-start = (f32[2,256]{1,0:T(2,128)S(1)}, f32[2,256]{1,0:T(2,128)}, u32[]{:S(2)}) copy-start(f32[2,256]{1,0:T(2,128)} %get-tuple-element.5) | copy-start | bytes 6148

commit v3 on v2

--- a/solution.py
+++ b/solution.py
@@ -42,17 +42,17 @@
     return jnp.concatenate([high, low, high, parts.astype(BF16)], axis=0)
 
 
-def invert_steps(matrix_ref, begin, end):
+def invert_steps(matrix_ref, begin, count):
     size = matrix_ref.shape[0]
     lane = lax.broadcasted_iota(jnp.int32, (size, LANES), 1)
     row_id = lax.broadcasted_iota(jnp.int32, (size, LANES), 0)
     lane_row = lax.broadcasted_iota(jnp.int32, (1, LANES), 1)
 
-    def step(j, carry):
+    for j in [begin + i for i in range(count)]:
         matrix = matrix_ref[...]
         row = matrix_ref[pl.ds(j, 1), :]
 
-        def pick(entries, ids):
+        def pick(entries, ids, j=j):
             first = jnp.sum(jnp.where(ids == j, entries, 0.0), axis=1, keepdims=True)
             second = jnp.sum(jnp.where(ids == j + size, entries, 0.0), axis=1, keepdims=True)
             return jnp.where(ids < size, first, second)
@@ -64,9 +64,6 @@
         reduced = jnp.where(here, -column * inverse, matrix - column * scaled)
         pivot_row = jnp.where(jnp.logical_or(lane_row == j, lane_row == j + size), inverse, scaled)
         matrix_ref[...] = jnp.where(row_id == j, pivot_row, reduced)
-        return carry
-
-    lax.fori_loop(begin, end, step, 0)
 
 
 def loop(begin, end, act):
@@ -202,7 +199,8 @@
             moment_ref[date * width : (date + 1) * width, cols] = high
             moment_ref[LANES + date * width : LANES + (date + 1) * width, cols] = low
 
-    loop(0, slots // size, moments)
+    blocks = slots // size
+    loop(0, blocks // 2, moments)
 
     loop(1, xys, lambda o: gram_copy(o).wait_recv())
     gram_sum[...] = jnp.sum(gram_in[...], axis=0)
@@ -215,6 +213,12 @@
 
     loop(1, xys, lambda o: gall_copy(o).start())
     gram_all[xy] = gram_sum[...]
+
+    loop(blocks // 2, blocks, moments)
+
+    loop(1, xys, lambda o: gall_wait(o).wait_recv())
+    for piece in range(xys):
+        matrix_ref[piece * rows : (piece + 1) * rows, :] = gram_all[piece, 0:rows, :]
 
     slot = core * slots + lax.broadcasted_iota(jnp.int32, (1, slots), 1)
     sets_ref[...] = jnp.where(slot < counts_ref[z], sets_ref[...], -1)
@@ -252,6 +256,7 @@
         row = lax.broadcasted_iota(jnp.int32, (set_count, slots), 0) + chunk * set_count
         member = jnp.where(row == sets_ref[...], notionals_ref[...], 0.0).astype(BF16)
         both = dot(member, moment_ref[...], 1, 1)
+        invert_steps(matrix_ref, chunk * (width // chunks), width // chunks)
         net_ref[owners(chunk)] = (both[:, :LANES] + both[:, LANES:]).reshape(per_chunk, *net_ref.shape[1:])
         core_copy(chunk).start()
 
@@ -281,14 +286,8 @@
         z_out[owners(chunk)] = jnp.sum(plane_in[:, owners(chunk)], axis=0)
         loop(chunk * per_chunk, (chunk + 1) * per_chunk, others(lambda to: z_copy(to).start()))
 
-    loop(0, chunks - 1, to_z)
-    loop(1, xys, lambda o: gall_wait(o).wait_recv())
-    for piece in range(xys):
-        matrix_ref[piece * rows : (piece + 1) * rows, :] = gram_all[piece, 0:rows, :]
-    invert_steps(matrix_ref, 0, width // 2)
-    to_z(chunks - 1)
+    loop(0, chunks, to_z)
     z_in[z] = z_out[z]
-    invert_steps(matrix_ref, width // 2, width)
     inverse = matrix_ref[...]
     left = lax.broadcasted_iota(jnp.int32, inverse.shape, 1) < width
     block = jnp.concatenate([jnp.where(left, inverse, 0.0), jnp.where(left, 0.0, inverse)], axis=0)

time: 62.1 us -> 58.1 us (0.936)
  Pallas kernels: 58.5 us -> 54.4 us
    pallas_call x1, Pallas kernels: 58.5 us -> 54.4 us  [body(): pl.pallas_call(functools.partial(kernel, zs, xys, size), out_shape=(jax.S...]
where the time goes in v3:
time: 58.1 us; the launch traced here: 57.9 us
  Pallas kernels  54.4 us (94%)
  local copies, waits for them, and re-layouts  2.85 us (5%)
  between operations  0.65 us (1%)
    pallas_call x1, Pallas kernels, body(): pl.pallas_call(functools.partial(kernel, zs, xys, size), out_shape=(jax.S...  54.4 us
    unnamed x4, local copies, waits for them, and re-layouts  2.85 us

profile of v3, /device:TPU:1, one launch (start us, length us, event | category | flops | bytes accessed | tf_op | source)
XLA Modules:
  0.0 57.9 jit_solution(14387762590794271584)
XLA Ops:
  0.6 54.4 %exposures.1 = (f32[2,256,512]{2,1,0:T(8,128)}, f32[2,256]{1,0:T(2,128)}) custom-call(f32[32,512]{1,0:T(8,128)} %bitcast.8, f32[2,32,512]{2,1,0:T(8,128)} %bitcast.7, s32[1,512]{1,0:T(1,128)} %bitcast.12, s32[1,256]{1,0:T(1,128)} %bitcast.13, s32[8]{0:T(128)} %counts_ref.1, f32[32,8192]{1,0:T(8,128)} %loadings_hbm.1, f32[1,8192]{1,0:T(1,128)} %bitcast.9, ...), custom_call_target="tpu_custom_call" | custom-call | tf_op jit(solution)/shard_map/exposures/pallas_call | solution.py:362
  55.1 0.0 copy-start
  55.1 2.3 %copy.13 = f32[2,256,512]{2,1,0:T(8,128)} copy(f32[2,256,512]{2,1,0:T(8,128)} %get-tuple-element.4) | data formatting | bytes 2097152
  57.4 0.0 copy-done
  57.4 0.6 copy.14
Async XLA Ops:
  55.1 2.3 %copy-start = (f32[2,256]{1,0:T(2,128)S(1)}, f32[2,256]{1,0:T(2,128)}, u32[]{:S(2)}) copy-start(f32[2,256]{1,0:T(2,128)} %get-tuple-element.5) | copy-start | bytes 6148

commit v4 on v3

v4 whole, which is shorter than its diff:
```python
import functools

import jax
import jax.numpy as jnp
from jax import lax
from jax.experimental import pallas as pl
from jax.experimental.pallas import tpu as pltpu
from jax.sharding import PartitionSpec as P

ROOT_HALF = 0.7071067811865476
F32, BF16 = jnp.float32, jnp.bfloat16
HIGHEST = lax.Precision.HIGHEST
MESH = pl.DeviceIdType.MESH
LANES = 128


def split(value):
    high = value.astype(BF16)
    return high, (value - high.astype(F32)).astype(BF16)


def dot(left, right, left_dim, right_dim, precision=None):
    return lax.dot_general(
        left, right, (((left_dim,), (right_dim,)), ((), ())), precision=precision, preferred_element_type=F32
    )


def make_basis(state):
    return jnp.concatenate([state, (state * state - 1.0) * ROOT_HALF], axis=0)


def scaled_trades(loadings_ref, strikes_ref, notionals_ref, block, size):
    cols = pl.ds(pl.multiple_of(block * size, size), size)
    scale = jnp.abs(notionals_ref[:, cols])
    high, low = split(loadings_ref[:, cols] * scale)
    strike = strikes_ref[:, cols] * (-scale)
    first = strike.astype(BF16).astype(F32)
    second = (strike - first).astype(BF16).astype(F32)
    third = (strike - first) - second
    row = lax.broadcasted_iota(jnp.int32, high.shape, 0)
    parts = jnp.where(row == 0, first, jnp.where(row == 1, second, jnp.where(row == 2, third, 0.0)))
    return jnp.concatenate([high, low, high, parts.astype(BF16)], axis=0)


def invert_steps(matrix_ref, begin, count):
    size = matrix_ref.shape[0]
    lane = lax.broadcasted_iota(jnp.int32, (size, LANES), 1)
    row_id = lax.broadcasted_iota(jnp.int32, (size, LANES), 0)
    lane_row = lax.broadcasted_iota(jnp.int32, (1, LANES), 1)

    for j in [begin + i for i in range(count)]:
        matrix = matrix_ref[...]
        row = matrix_ref[pl.ds(j, 1), :]

        def pick(entries, ids, j=j):
            first = jnp.sum(jnp.where(ids == j, entries, 0.0), axis=1, keepdims=True)
            second = jnp.sum(jnp.where(ids == j + size, entries, 0.0), axis=1, keepdims=True)
            return jnp.where(ids < size, first, second)

        column = pick(matrix, lane)
        inverse = 1.0 / pick(row, lane_row)
        scaled = row * inverse
        here = jnp.logical_or(lane == j, lane == j + size)
        reduced = jnp.where(here, -column * inverse, matrix - column * scaled)
        pivot_row = jnp.where(jnp.logical_or(lane_row == j, lane_row == j + size), inverse, scaled)
        matrix_ref[...] = jnp.where(row_id == j, pivot_row, reduced)


def loop(begin, end, act):
    def step(i, carry):
        act(i)
        return carry

    lax.fori_loop(begin, end, step, 0)


def kernel(
    zs, xys, size,
    start_hbm, shocks_hbm, weights_hbm, thresholds_hbm, counts_ref, loadings_hbm, strikes_hbm, notionals_hbm, sets_hbm,
    exposure_ref, expected_ref,
    start_ref, shocks_ref, weights_ref, thresholds_ref,
    loadings_ref, strikes_ref, notionals_ref, sets_ref, local_sem, out_ref, out_sem,
    own_states, other_states, state_ref, wbasis_ref, basis_ref, total_ref, moment_ref,
    gram_out, gram_in, gram_sum, gram_all, matrix_ref,
    net_ref, core_in, plane_out, plane_in, z_out, z_in, own_ref, coeffs_ref, part_ref,
    state_send, state_recv, gram_send, gram_recv, gall_send, gall_recv, core_send, core_recv, plane_send, plane_recv,
    z_send, z_recv, coeff_send, coeff_recv, part_send, part_recv,
):
    z = lax.axis_index("trade")
    q = lax.axis_index("path")
    xy, core = q // 2, lax.rem(q, 2)
    other = 1 - core
    qs = 2 * xys
    factors, paths = start_ref.shape
    dates = shocks_ref.shape[0]
    width = 2 * factors
    slots = loadings_ref.shape[1]
    chunks = core_send.shape[0]
    per_chunk = zs // chunks
    set_count = per_chunk * thresholds_ref.shape[1]

    def copy(src, dst, send, recv, device):
        return pltpu.make_async_remote_copy(
            src_ref=src, dst_ref=dst, send_sem=send, recv_sem=recv, device_id=device, device_id_type=MESH
        )

    def target(cores, o):
        return (z, lax.rem(q + o, qs) if cores == 2 else lax.rem(xy + o, xys) * 2 + core)

    def wait_all(ref, send, recv):
        copy(ref, ref, send, recv, target(2, 1)).wait_recv()

    def sent_all(ref, send, recv):
        copy(ref, ref, send, recv, target(2, 1)).wait_send()

    def around(cores, act):
        loop(1, cores * xys, lambda o: act(o, cores, o))

    half = pl.ds(pl.multiple_of(core * slots, slots), slots)
    fetches = [
        pltpu.make_async_copy(hbm.at[:, half], ref, local_sem.at[i])
        for i, (hbm, ref) in enumerate(
            [
                (loadings_hbm, loadings_ref),
                (strikes_hbm, strikes_ref),
                (notionals_hbm, notionals_ref),
                (sets_hbm, sets_ref),
            ]
        )
    ]
    firsts = [
        pltpu.make_async_copy(hbm, ref, local_sem.at[len(fetches) + i])
        for i, (hbm, ref) in enumerate(
            [
                (start_hbm, start_ref),
                (shocks_hbm, shocks_ref),
                (weights_hbm, weights_ref),
                (thresholds_hbm, thresholds_ref),
            ]
        )
    ]
    for fetch in firsts + fetches:
        fetch.start()

    barrier = pltpu.get_barrier_semaphore()

    def greet(device):
        pl.semaphore_signal(barrier, inc=1, device_id=device, device_id_type=MESH)

    loop(1, qs, lambda o: greet((z, lax.rem(q + o, qs))))
    loop(1, zs, lambda o: greet((lax.rem(z + o, zs), q)))

    for fetch in firsts:
        fetch.wait()
    weight = jnp.broadcast_to(weights_ref[...].astype(F32), (8, paths))
    state = start_ref[...]
    own_states[0:factors, :] = state
    for date in range(dates):
        state = 0.8 * state + 0.6 * shocks_ref[date]
        own_states[(date + 1) * factors : (date + 2) * factors, :] = state
    bottom = (dates + 1) * factors
    own_states[bottom : bottom + 8, :] = weight

    def prepare(states, place):
        scale = states[bottom : bottom + 1, :]
        grams = []
        for date in range(dates):
            basis = make_basis(states[date * factors : (date + 1) * factors, :])
            weighted = basis * scale
            high, low = split(weighted)
            wbasis_ref[place, date, 0:width, :] = high
            wbasis_ref[place, date, width : 2 * width, :] = low
            future = states[(date + 1) * factors : (date + 2) * factors, :]
            high = future.astype(BF16).astype(F32)
            ones = jnp.where(lax.broadcasted_iota(jnp.int32, future.shape, 0) < 3, 1.0, 0.0)
            rows = jnp.concatenate([high, high, future - high, ones], axis=0)
            state_ref[place, date] = rows.T.astype(BF16)
            if place == 0:
                grams.append(dot(weighted, basis, 1, 1, HIGHEST))
                high, low = split(basis)
                zero = jnp.zeros_like(high)
                for part, entries in enumerate((high, high, low)):
                    for k in range(dates):
                        at = part * dates * width + k * width
                        basis_ref[date, at : at + width, :] = entries if k == date else zero
        return grams

    def moments(block, place):
        trades = scaled_trades(loadings_ref, strikes_ref, notionals_ref, block, size)
        cols = pl.ds(pl.multiple_of(block * size, size), size)
        for date in range(dates):
            flows = jnp.maximum(dot(state_ref[place, date], trades, 1, 0), 0.0)
            high, low = split(flows)
            both = dot(wbasis_ref[place, date], high, 1, 0)
            least = dot(wbasis_ref[place, date, 0:width, :], low, 1, 0)
            moment = both[0:width] + both[width:] + least
            at = date * width
            if place == 0:
                total_ref[at : at + width, cols] = moment
            else:
                high, low = split(moment + total_ref[at : at + width, cols])
                moment_ref[at : at + width, cols] = high
                moment_ref[LANES + at : LANES + at + width, cols] = low

    gram = jnp.concatenate(prepare(own_states, 0), axis=1)
    rows = width // qs
    for piece in range(qs):
        gram_out[piece, 0:rows, :] = gram[piece * rows : (piece + 1) * rows, :]
        gram_out[piece, rows : rows + 1, :] = jnp.broadcast_to(jnp.sum(weight[0:1, :], axis=1, keepdims=True), (1, LANES))
    for fetch in fetches:
        fetch.wait()
    blocks = slots // size
    loop(0, blocks - 1, lambda block: moments(block, 0))

    pl.semaphore_wait(barrier, qs - 1 + zs - 1)
    states_copy = copy(own_states, other_states, state_send, state_recv, (z, xy * 2 + other))
    states_copy.start()

    def gram_copy(o, *offset):
        to = target(*offset)
        return copy(gram_out.at[to[1]], gram_in.at[o], gram_send, gram_recv, to)

    around(2, lambda *at: gram_copy(*at).start())
    gram_in[0] = gram_out[q]
    moments(blocks - 1, 0)

    states_copy.wait_recv()
    prepare(other_states, 1)
    loop(0, blocks - 1, lambda block: moments(block, 1))

    wait_all(gram_in.at[1:qs], gram_send, gram_recv)
    gram_sum[...] = jnp.sum(gram_in[...], axis=0)

    def gall_copy(o, *offset):
        return copy(gram_sum, gram_all.at[q], gall_send, gall_recv, target(*offset))

    around(2, lambda *at: gall_copy(*at).start())
    gram_all[q] = gram_sum[...]
    moments(blocks - 1, 1)

    slot = core * slots + lax.broadcasted_iota(jnp.int32, (1, slots), 1)
    sets_ref[...] = jnp.where(slot < counts_ref[z], sets_ref[...], -1)
    notional = notionals_ref[...]
    notionals_ref[...] = jnp.where(notional > 0, 1.0, jnp.where(notional < 0, -1.0, 0.0))

    def owners(chunk):
        return pl.ds(chunk * per_chunk, per_chunk)

    def core_copy(chunk):
        return copy(
            net_ref.at[owners(chunk), other],
            core_in.at[owners(chunk)],
            core_send.at[chunk],
            core_recv.at[chunk],
            (z, xy * 2 + other),
        )

    def plane_copy(chunk, o, *offset):
        to = target(*offset)
        return copy(
            plane_out.at[owners(chunk), to[1] // 2],
            plane_in.at[o, owners(chunk)],
            plane_send.at[chunk],
            plane_recv.at[chunk],
            to,
        )

    def to_plane(chunk):
        core_copy(chunk).wait_recv()
        plane_out[owners(chunk)] = net_ref[owners(chunk), core] + core_in[owners(chunk)]
        around(1, lambda *at: plane_copy(chunk, *at).start())
        plane_in[0, owners(chunk)] = plane_out[owners(chunk), xy]

    def turn(i):
        return lax.rem(z // per_chunk + 1 + i, chunks)

    few = width * 3 // 16

    def more_steps(begin, count):
        loop(0, count // 4, lambda i: invert_steps(matrix_ref, begin + i * 4, 4))

    def net(i, first=False, begin=None):
        chunk = turn(i)
        row = lax.broadcasted_iota(jnp.int32, (set_count, slots), 0) + chunk * set_count
        member = jnp.where(row == sets_ref[...], notionals_ref[...], 0.0).astype(BF16)
        both = dot(member, moment_ref[...], 1, 1)
        if begin is not None:
            invert_steps(matrix_ref, begin, few)
        net_ref[owners(chunk)] = (both[:, :LANES] + both[:, LANES:]).reshape(per_chunk, *net_ref.shape[1:])
        core_copy(chunk).start()
        if not first:
            to_plane(turn(i - 1))

    net(0, True)
    loop(1, chunks - 2, net)
    wait_all(gram_all.at[1:qs], gall_send, gall_recv)
    for piece in range(qs):
        matrix_ref[piece * rows : (piece + 1) * rows, :] = gram_all[piece, 0:rows, :]
    loop(chunks - 2, chunks, lambda i: net(i, False, (i - chunks + 2) * few))
    to_plane(turn(chunks - 1))

    def z_copy(to):
        return copy(z_out.at[to], z_in.at[z], z_send, z_recv, (to, q))

    def others(act):
        def one(to):
            @pl.when(to != z)
            def _():
                act(to)

        return one

    def to_z(chunk):
        wait_all(plane_in.at[1:xys, owners(chunk)], plane_send.at[chunk], plane_recv.at[chunk])
        z_out[owners(chunk)] = jnp.sum(plane_in[:, owners(chunk)], axis=0)
        loop(chunk * per_chunk, (chunk + 1) * per_chunk, others(lambda to: z_copy(to).start()))

    loop(0, chunks - 2, lambda i: to_z(turn(i)))
    more_steps(2 * few, width - 4 * few)
    to_z(turn(chunks - 2))
    more_steps(width - 2 * few, few)
    to_z(turn(chunks - 1))
    z_in[z] = z_out[z]
    more_steps(width - few, few)
    inverse = matrix_ref[...]
    left = lax.broadcasted_iota(jnp.int32, inverse.shape, 1) < width
    block = jnp.concatenate([jnp.where(left, inverse, 0.0), jnp.where(left, 0.0, inverse)], axis=0)
    wait_all(z_in.at[1:zs], z_send, z_recv)
    own_ref[...] = dot(jnp.sum(z_in[...], axis=0), block, 1, 0, HIGHEST)

    mine = core * xys + xy

    def coeff_copy(o, *offset):
        return copy(own_ref, coeffs_ref.at[mine], coeff_send, coeff_recv, target(*offset))

    around(2, lambda *at: coeff_copy(*at).start())
    coeffs_ref[mine] = own_ref[...]
    sets = thresholds_ref.shape[1]
    limits = jnp.broadcast_to(0.25 * thresholds_ref[...].astype(F32), (LANES, sets)).T
    wait_all(coeffs_ref.at[1:qs], coeff_send, coeff_recv)

    high, low = split(coeffs_ref[...].reshape(sets, LANES))
    coeffs = jnp.concatenate([high, low, high], axis=1)
    weight = weight.astype(BF16)
    for date in range(dates):
        exposure = jnp.maximum(dot(coeffs, basis_ref[date], 1, 0) - limits[:, 0:1], 0.0)
        out_ref[date] = exposure
        high, low = split(exposure)
        part = dot(weight, high, 1, 1) + dot(weight, low, 1, 1)
        part_ref[q, date : date + 1, :] = part[0:1, :]

    def part_copy(o, *offset):
        return copy(part_ref.at[q], part_ref.at[q], part_send, part_recv, target(*offset))

    around(2, lambda *at: part_copy(*at).start())
    out_copy = pltpu.make_async_copy(out_ref, exposure_ref, out_sem)
    out_copy.start()
    states_copy.wait_send()
    sent_all(gram_in.at[1:qs], gram_send, gram_recv)
    sent_all(gram_all.at[1:qs], gall_send, gall_recv)
    loop(0, chunks, lambda chunk: core_copy(chunk).wait_send())
    loop(
        0, chunks, lambda chunk: sent_all(plane_in.at[1:xys, owners(chunk)], plane_send.at[chunk], plane_recv.at[chunk])
    )
    sent_all(z_in.at[1:zs], z_send, z_recv)
    sent_all(coeffs_ref.at[1:qs], coeff_send, coeff_recv)
    out_copy.wait()
    wait_all(part_ref.at[1:qs], part_send, part_recv)
    expected_ref[...] = jnp.sum(part_ref[...], axis=0) / gram_all[0, rows : rows + 1, 0:1]
    sent_all(part_ref.at[1:qs], part_send, part_recv)


def body(
    start_state, shocks, loadings, strikes, notionals, trade_set, live_counts, weights, thresholds
):
    zs, qs = lax.axis_size("trade"), lax.axis_size("path")
    xys = qs // 2
    paths, factors = start_state.shape
    dates = shocks.shape[0]
    width = 2 * factors
    slots = loadings.shape[1] // 2
    size = min(1024, slots)
    sets = thresholds.shape[0]
    per = sets // qs
    chunks = 4 if zs % 4 == 0 else zs
    tall = (width // qs + 8) // 8 * 8
    vmem = pl.BlockSpec(memory_space=pltpu.VMEM)
    hbm = pl.BlockSpec(memory_space=pl.ANY)
    dma = pltpu.SemaphoreType.DMA
    return pl.pallas_call(
        functools.partial(kernel, zs, xys, size),
        out_shape=(
            jax.ShapeDtypeStruct((dates, sets, paths), F32),
            jax.ShapeDtypeStruct((dates, sets), F32),
        ),
        in_specs=[hbm] * 4 + [pl.BlockSpec(memory_space=pltpu.SMEM)] + [hbm] * 4,
        out_specs=(hbm, vmem),
        scratch_shapes=[
            pltpu.VMEM((factors, paths), F32),
            pltpu.VMEM((dates, factors, paths), F32),
            pltpu.VMEM((1, paths), jnp.int32),
            pltpu.VMEM((1, sets), jnp.int32),
            pltpu.VMEM((factors, slots), F32),
            pltpu.VMEM((1, slots), F32),
            pltpu.VMEM((1, slots), F32),
            pltpu.VMEM((1, slots), jnp.int32),
            dma((8,)),
            pltpu.VMEM((dates, sets, paths), F32),
            dma,
            pltpu.VMEM(((dates + 1) * factors + 8, paths), F32),
            pltpu.VMEM(((dates + 1) * factors + 8, paths), F32),
            pltpu.VMEM((2, dates, paths, 4 * factors), BF16),
            pltpu.VMEM((2, dates, 2 * width, paths), BF16),
            pltpu.VMEM((dates, 3 * dates * width, paths), BF16),
            pltpu.VMEM((LANES, slots), F32),
            pltpu.VMEM((2 * LANES, slots), BF16),
            pltpu.VMEM((qs, tall, LANES), F32),
            pltpu.VMEM((qs, tall, LANES), F32),
            pltpu.VMEM((tall, LANES), F32),
            pltpu.VMEM((qs, tall, LANES), F32),
            pltpu.VMEM((width, LANES), F32),
            pltpu.VMEM((zs, 2, xys, per, LANES), F32),
            pltpu.VMEM((zs, xys, per, LANES), F32),
            pltpu.VMEM((zs, xys, per, LANES), F32),
            pltpu.VMEM((xys, zs, per, LANES), F32),
            pltpu.VMEM((zs, per, LANES), F32),
            pltpu.VMEM((zs, per, LANES), F32),
            pltpu.VMEM((per, LANES), F32),
            pltpu.VMEM((qs, per, LANES), F32),
            pltpu.VMEM((qs, dates, sets), F32),
            dma, dma, dma, dma, dma, dma, dma((chunks,)), dma((chunks,)), dma((chunks,)), dma((chunks,)),
            dma, dma, dma, dma, dma, dma,
        ],
        compiler_params=pltpu.CompilerParams(
            collective_id=0, has_side_effects=True, vmem_limit_bytes=56 << 20
        ),
        name="exposures",
    )(
        start_state.T, shocks.transpose(0, 2, 1), weights.reshape(1, -1), thresholds.reshape(1, -1), live_counts,
        loadings, strikes.reshape(1, -1), notionals.reshape(1, -1), trade_set.reshape(1, -1),
    )


def solution(mesh):
    placed = (
        P("path", None),
        P(None, "path", None),
        P(None, "trade"),
        P("trade"),
        P("trade"),
        P("trade"),
        P(),
        P("path"),
        P("trade"),
    )
    return jax.shard_map(
        body,
        mesh=mesh,
        in_specs=placed,
        out_specs=(P(None, "trade", "path"), P(None, "trade")),
        check_vma=False,
    )
```

time: 58.1 us -> 53.6 us (0.923)
  Pallas kernels: 54.4 us -> 50 us
    pallas_call x1, Pallas kernels: 54.4 us -> 50 us  [body(): pl.pallas_call(functools.partial(kernel, zs, xys, size), out_shape=(jax.S...]
where the time goes in v4:
time: 53.6 us; the launch traced here: 53.5 us
  Pallas kernels  50 us (93%)
  local copies, waits for them, and re-layouts  2.85 us (5%)
  between operations  0.65 us (1%)
    pallas_call x1, Pallas kernels, body(): pl.pallas_call(functools.partial(kernel, zs, xys, size), out_shape=(jax.S...  50 us
    unnamed x4, local copies, waits for them, and re-layouts  2.85 us

profile of v4, /device:TPU:1, one launch (start us, length us, event | category | flops | bytes accessed | tf_op | source)
XLA Modules:
  0.0 53.5 jit_solution(15025533280468358318)
XLA Ops:
  0.6 50.0 %exposures.1 = (f32[2,256,512]{2,1,0:T(8,128)}, f32[2,256]{1,0:T(2,128)}) custom-call(f32[32,512]{1,0:T(8,128)} %bitcast.8, f32[2,32,512]{2,1,0:T(8,128)} %bitcast.7, s32[1,512]{1,0:T(1,128)} %bitcast.12, s32[1,256]{1,0:T(1,128)} %bitcast.13, s32[8]{0:T(128)} %counts_ref.1, f32[32,8192]{1,0:T(8,128)} %loadings_hbm.1, f32[1,8192]{1,0:T(1,128)} %bitcast.9, ...), custom_call_target="tpu_custom_call" | custom-call | tf_op jit(solution)/shard_map/exposures/pallas_call | solution.py:390
  50.6 0.0 copy-start
  50.6 2.3 %copy.13 = f32[2,256,512]{2,1,0:T(8,128)} copy(f32[2,256,512]{2,1,0:T(8,128)} %get-tuple-element.4) | data formatting | bytes 2097152
  52.9 0.0 copy-done
  52.9 0.6 %copy.14 = f32[2,256]{1,0:T(2,128)} copy(f32[2,256]{1,0:T(2,128)S(1)} %copy-done) | data formatting | bytes 4096
Async XLA Ops:
  50.6 2.3 %copy-start = (f32[2,256]{1,0:T(2,128)S(1)}, f32[2,256]{1,0:T(2,128)}, u32[]{:S(2)}) copy-start(f32[2,256]{1,0:T(2,128)} %get-tuple-element.5) | copy-start | bytes 6148

commit v5 on v4

--- a/solution.py
+++ b/solution.py
@@ -275,6 +275,8 @@
         return lax.rem(z // per_chunk + 1 + i, chunks)
 
     few = width * 3 // 16
+    late = chunks // 2
+    beside = 2 * few // late
 
     def more_steps(begin, count):
         loop(0, count // 4, lambda i: invert_steps(matrix_ref, begin + i * 4, 4))
@@ -285,18 +287,18 @@
         member = jnp.where(row == sets_ref[...], notionals_ref[...], 0.0).astype(BF16)
         both = dot(member, moment_ref[...], 1, 1)
         if begin is not None:
-            invert_steps(matrix_ref, begin, few)
+            invert_steps(matrix_ref, begin, beside)
         net_ref[owners(chunk)] = (both[:, :LANES] + both[:, LANES:]).reshape(per_chunk, *net_ref.shape[1:])
         core_copy(chunk).start()
         if not first:
             to_plane(turn(i - 1))
 
     net(0, True)
-    loop(1, chunks - 2, net)
+    loop(1, chunks - late, net)
     wait_all(gram_all.at[1:qs], gall_send, gall_recv)
     for piece in range(qs):
         matrix_ref[piece * rows : (piece + 1) * rows, :] = gram_all[piece, 0:rows, :]
-    loop(chunks - 2, chunks, lambda i: net(i, False, (i - chunks + 2) * few))
+    loop(chunks - late, chunks, lambda i: net(i, False, (i - chunks + late) * beside))
     to_plane(turn(chunks - 1))
 
     def z_copy(to):
@@ -382,7 +384,7 @@
     size = min(1024, slots)
     sets = thresholds.shape[0]
     per = sets // qs
-    chunks = 4 if zs % 4 == 0 else zs
+    chunks = zs
     tall = (width // qs + 8) // 8 * 8
     vmem = pl.BlockSpec(memory_space=pltpu.VMEM)
     hbm = pl.BlockSpec(memory_space=pl.ANY)

time: 53.6 us -> 52.8 us (0.985)
  Pallas kernels: 50 us -> 49.2 us
    pallas_call x1, Pallas kernels: 50 us -> 49.2 us  [body(): pl.pallas_call(functools.partial(kernel, zs, xys, size), out_shape=(jax.S...]
where the time goes in v5:
time: 52.8 us; the launch traced here: 52.7 us
  Pallas kernels  49.2 us (93%)
  local copies, waits for them, and re-layouts  2.85 us (5%)
  between operations  0.65 us (1%)
    pallas_call x1, Pallas kernels, body(): pl.pallas_call(functools.partial(kernel, zs, xys, size), out_shape=(jax.S...  49.2 us
    unnamed x4, local copies, waits for them, and re-layouts  2.85 us

profile of v5, /device:TPU:1, one launch (start us, length us, event | category | flops | bytes accessed | tf_op | source)
XLA Modules:
  0.0 52.7 jit_solution(11096797011725224655)
XLA Ops:
  0.6 49.2 %exposures.1 = (f32[2,256,512]{2,1,0:T(8,128)}, f32[2,256]{1,0:T(2,128)}) custom-call(f32[32,512]{1,0:T(8,128)} %bitcast.8, f32[2,32,512]{2,1,0:T(8,128)} %bitcast.7, s32[1,512]{1,0:T(1,128)} %bitcast.12, s32[1,256]{1,0:T(1,128)} %bitcast.13, s32[8]{0:T(128)} %counts_ref.1, f32[32,8192]{1,0:T(8,128)} %loadings_hbm.1, f32[1,8192]{1,0:T(1,128)} %bitcast.9, ...), custom_call_target="tpu_custom_call" | custom-call | tf_op jit(solution)/shard_map/exposures/pallas_call | solution.py:392
  49.9 0.0 copy-start
  49.9 2.3 %copy.13 = f32[2,256,512]{2,1,0:T(8,128)} copy(f32[2,256,512]{2,1,0:T(8,128)} %get-tuple-element.4) | data formatting | bytes 2097152
  52.1 0.0 copy-done
  52.1 0.6 %copy.14 = f32[2,256]{1,0:T(2,128)} copy(f32[2,256]{1,0:T(2,128)S(1)} %copy-done) | data formatting | bytes 4096
Async XLA Ops:
  49.9 2.3 %copy-start = (f32[2,256]{1,0:T(2,128)S(1)}, f32[2,256]{1,0:T(2,128)}, u32[]{:S(2)}) copy-start(f32[2,256]{1,0:T(2,128)} %get-tuple-element.5) | copy-start | bytes 6148

commit v6 on v5

--- a/solution.py
+++ b/solution.py
@@ -77,9 +77,9 @@
 def kernel(
     zs, xys, size,
     start_hbm, shocks_hbm, weights_hbm, thresholds_hbm, counts_ref, loadings_hbm, strikes_hbm, notionals_hbm, sets_hbm,
-    exposure_ref, expected_ref,
+    result_ref, expected_ref,
     start_ref, shocks_ref, weights_ref, thresholds_ref,
-    loadings_ref, strikes_ref, notionals_ref, sets_ref, local_sem, out_ref, out_sem,
+    loadings_ref, strikes_ref, notionals_ref, sets_ref, local_sem,
     own_states, other_states, state_ref, wbasis_ref, basis_ref, total_ref, moment_ref,
     gram_out, gram_in, gram_sum, gram_all, matrix_ref,
     net_ref, core_in, plane_out, plane_in, z_out, z_in, own_ref, coeffs_ref, part_ref,
@@ -346,7 +346,6 @@
     weight = weight.astype(BF16)
     for date in range(dates):
         exposure = jnp.maximum(dot(coeffs, basis_ref[date], 1, 0) - limits[:, 0:1], 0.0)
-        out_ref[date] = exposure
         high, low = split(exposure)
         part = dot(weight, high, 1, 1) + dot(weight, low, 1, 1)
         part_ref[q, date : date + 1, :] = part[0:1, :]
@@ -355,8 +354,7 @@
         return copy(part_ref.at[q], part_ref.at[q], part_send, part_recv, target(*offset))
 
     around(2, lambda *at: part_copy(*at).start())
-    out_copy = pltpu.make_async_copy(out_ref, exposure_ref, out_sem)
-    out_copy.start()
+    result_ref[...] = coeffs_ref[...]
     states_copy.wait_send()
     sent_all(gram_in.at[1:qs], gram_send, gram_recv)
     sent_all(gram_all.at[1:qs], gall_send, gall_recv)
@@ -366,10 +364,24 @@
     )
     sent_all(z_in.at[1:zs], z_send, z_recv)
     sent_all(coeffs_ref.at[1:qs], coeff_send, coeff_recv)
-    out_copy.wait()
     wait_all(part_ref.at[1:qs], part_send, part_recv)
     expected_ref[...] = jnp.sum(part_ref[...], axis=0) / gram_all[0, rows : rows + 1, 0:1]
     sent_all(part_ref.at[1:qs], part_send, part_recv)
+
+
+def exposure_kernel(coeffs_ref, start_ref, shocks_ref, thresholds_ref, exposure_ref):
+    dates, sets, _ = exposure_ref.shape
+    width = 2 * start_ref.shape[0]
+    high, low = split(coeffs_ref[...].reshape(sets, LANES))
+    coeffs = jnp.concatenate([high, low, high], axis=1)
+    limits = jnp.broadcast_to(0.25 * thresholds_ref[...].astype(F32), (LANES, sets)).T
+    state = start_ref[...]
+    for date in range(dates):
+        high, low = split(make_basis(state))
+        zero = jnp.zeros_like(high)
+        parts = [entries if k == date else zero for entries in (high, high, low) for k in range(dates)]
+        exposure_ref[date] = jnp.maximum(dot(coeffs, jnp.concatenate(parts, axis=0), 1, 0) - limits[:, 0:1], 0.0)
+        state = 0.8 * state + 0.6 * shocks_ref[date]
 
 
 def body(
@@ -389,14 +401,14 @@
     vmem = pl.BlockSpec(memory_space=pltpu.VMEM)
     hbm = pl.BlockSpec(memory_space=pl.ANY)
     dma = pltpu.SemaphoreType.DMA
-    return pl.pallas_call(
+    coeffs, expected = pl.pallas_call(
         functools.partial(kernel, zs, xys, size),
         out_shape=(
-            jax.ShapeDtypeStruct((dates, sets, paths), F32),
+            jax.ShapeDtypeStruct((qs, per, LANES), F32),
             jax.ShapeDtypeStruct((dates, sets), F32),
         ),
         in_specs=[hbm] * 4 + [pl.BlockSpec(memory_space=pltpu.SMEM)] + [hbm] * 4,
-        out_specs=(hbm, vmem),
+        out_specs=(vmem, vmem),
         scratch_shapes=[
             pltpu.VMEM((factors, paths), F32),
             pltpu.VMEM((dates, factors, paths), F32),
@@ -407,8 +419,6 @@
             pltpu.VMEM((1, slots), F32),
             pltpu.VMEM((1, slots), jnp.int32),
             dma((8,)),
-            pltpu.VMEM((dates, sets, paths), F32),
-            dma,
             pltpu.VMEM(((dates + 1) * factors + 8, paths), F32),
             pltpu.VMEM(((dates + 1) * factors + 8, paths), F32),
             pltpu.VMEM((2, dates, paths, 4 * factors), BF16),
@@ -441,6 +451,15 @@
         start_state.T, shocks.transpose(0, 2, 1), weights.reshape(1, -1), thresholds.reshape(1, -1), live_counts,
         loadings, strikes.reshape(1, -1), notionals.reshape(1, -1), trade_set.reshape(1, -1),
     )
+    exposure = pl.pallas_call(
+        exposure_kernel,
+        out_shape=jax.ShapeDtypeStruct((dates, sets, paths), F32),
+        in_specs=[vmem] * 4,
+        out_specs=vmem,
+        compiler_params=pltpu.CompilerParams(vmem_limit_bytes=56 << 20),
+        name="exposure",
+    )(coeffs, start_state.T, shocks.transpose(0, 2, 1), thresholds.reshape(1, -1))
+    return exposure, expected
 
 
 def solution(mesh):

time: 52.8 us -> 53.1 us (level)
  Pallas kernels: 49.2 us -> 51.7 us
  local copies, waits for them, and re-layouts: 2.85 us -> 0.58 us
    pallas_call x0 -> x1, Pallas kernels: none -> 2.42 us  [body(): pl.pallas_call(exposure_kernel, out_shape=jax.ShapeDtypeStruct((dates, se...]
    unnamed x4 -> x3, local copies, waits for them, and re-layouts: 2.85 us -> 0.58 us
where the time goes in v6:
time: 53.1 us; the launch traced here: 52.9 us
  Pallas kernels  51.7 us (97%)
  between operations  0.65 us (1%)
  local copies, waits for them, and re-layouts  0.58 us (1%)
    pallas_call x1, Pallas kernels, body(): pl.pallas_call(functools.partial(kernel, zs, xys, size), out_shape=(jax.S...  49.3 us
    pallas_call x1, Pallas kernels, body(): pl.pallas_call(exposure_kernel, out_shape=jax.ShapeDtypeStruct((dates, se...  2.42 us

profile of v6, /device:TPU:1, one launch (start us, length us, event | category | flops | bytes accessed | tf_op | source)
XLA Modules:
  0.0 52.9 jit_solution(12220323352804448583)
XLA Ops:
  0.6 49.3 %exposures.1 = (f32[32,8,128]{2,1,0:T(8,128)}, f32[2,256]{1,0:T(2,128)}) custom-call(f32[32,512]{1,0:T(8,128)} %bitcast.9, f32[2,32,512]{2,1,0:T(8,128)} %bitcast.7, s32[1,512]{1,0:T(1,128)} %bitcast.16, s32[1,256]{1,0:T(1,128)} %bitcast.14, s32[8]{0:T(128)} %counts_ref.1, f32[32,8192]{1,0:T(8,128)} %loadings_hbm.1, f32[1,8192]{1,0:T(1,128)} %bitcast.11, ...), custom_call_target="tpu_custom_call" | custom-call | tf_op jit(solution)/shard_map/exposures/pallas_call | solution.py:404
  49.9 0.0 copy-start
  49.9 2.4 %exposure.1 = f32[2,256,512]{2,1,0:T(8,128)} custom-call(f32[32,8,128]{2,1,0:T(8,128)} %get-tuple-element.4.coeffs_ref, f32[32,512]{1,0:T(8,128)} %bitcast.10, f32[2,32,512]{2,1,0:T(8,128)} %bitcast.8, s32[1,256]{1,0:T(1,128)} %bitcast.15), custom_call_target="tpu_custom_call" | custom-call | tf_op jit(solution)/shard_map/exposure/pallas_call | solution.py:454
  52.3 0.0 copy-done
  52.3 0.6 %copy.12 = f32[2,256]{1,0:T(2,128)} copy(f32[2,256]{1,0:T(2,128)S(1)} %copy-done) | data formatting | bytes 4096
Async XLA Ops:
  49.9 2.4 %copy-start = (f32[2,256]{1,0:T(2,128)S(1)}, f32[2,256]{1,0:T(2,128)}, u32[]{:S(2)}) copy-start(f32[2,256]{1,0:T(2,128)} %get-tuple-element.9) | copy-start | bytes 6148
